TPU v7x, 512 devices: a whole 4x8x8 slice. The times are simulated.
512 devices in a mesh: dp: 128 (over z, y, core), grp: 4 (over x).
Axes of the slice: x: 4, y: 8, z: 8, core: 2. Of those that a mesh axis runs over, the one named last changes fastest.
Arguments:
- features: bfloat16 [65536, 512], P(('dp', 'grp'))
- loss_scale: bfloat16 [65536], P(('dp', 'grp')), may hold values from 8 to 32
- blocks: int32 [65536, 8], P(('dp', 'grp')), may hold values from 0 to 511, all different within a row; in each aligned block of 128 rows (0 to 127, 128 to 255, ...) at most 3 rows name the same one
- label_col: int32 [65536], P(('dp', 'grp')), may hold values from 0 to 1023
- block_slot: int32 [512], replicated, may hold values from 0 to 511, each once
- centers: bfloat16 [524288, 512], P(('dp', 'grp'))
Outputs:
- loss_out: float32 [65536], P(('dp', 'grp'))
- feature_grad: float32 [65536, 512], P(('dp', 'grp'))
- center_grad: bfloat16 [524288, 512], P(('dp', 'grp'))
Inputs may be any that keep to these rules, and one draw needn't show every extreme that they name: Each row names 8 different blocks; the first is the sample's own block. Among the rows of one device no block is named by more than 3 rows, and some block is named by exactly 3. A permutation: block b is stored in rows block_slot[b] * 1024 to block_slot[b] * 1024 + 1023 of centers.
All inputs are finite; a program needn't handle non-finite values.
Results may differ from a plain program's by a relative error of at most 0.0054.
Values may be sent and summed in bfloat16 or wider, within the bound.
No kernel may reach another device: no remote copies, remote signals or barrier semaphores. Data moves between devices by JAX's collectives and lax.ppermute only.
A program may use at most 64 MiB of HBM per device.

v0:
```python
import jax
import jax.numpy as jnp
from jax import lax
from jax.experimental import pallas as pl
from jax.experimental.pallas import tpu as pltpu
from jax.sharding import PartitionSpec as P

BLOCK = 1024
MOST = 3
LANES = 128
MARGIN = 0.35
LOGIT_SCALE = 64.0
EPSILON = 1e-06
AXES = ("dp", "grp")

VMEM = pl.BlockSpec(memory_space=pltpu.VMEM)


def nt_dot(a, b):
    return lax.dot_general(a, b, (((1,), (1,)), ((), ())), preferred_element_type=jnp.float32)


def tn_dot(a, b):
    return lax.dot_general(a, b, (((0,), (0,)), ((), ())), preferred_element_type=jnp.float32)


def nn_dot(a, b):
    return jnp.dot(a, b, preferred_element_type=jnp.float32)


def call(kernel, outs, scratch=(), name=None):
    return pl.pallas_call(
        kernel,
        out_shape=outs,
        scratch_shapes=list(scratch),
        compiler_params=pltpu.CompilerParams(vmem_limit_bytes=56 * 1024 * 1024),
        name=name,
    )


def dispatch_kernel(feat_ref, blocks_ref, label_ref, slot_ref, pay_ref, sel_ref, stage):
    samples, width = feat_ref.shape
    total = slot_ref.shape[1]
    segs = width // LANES
    rows = MOST * segs + 2
    x = feat_ref[...].astype(jnp.float32)
    norm = jnp.sqrt(jnp.sum(x * x, axis=1, keepdims=True) + EPSILON)
    normed = (x / norm).astype(jnp.bfloat16)
    named_by = blocks_ref[...]
    block_iota = lax.broadcasted_iota(jnp.int32, (samples, total), 1)
    own = named_by[:, 0:1] == block_iota
    named = own
    for k in range(1, blocks_ref.shape[1]):
        named = named | (named_by[:, k : k + 1] == block_iota)
    one_hot = (lax.broadcasted_iota(jnp.int32, (total, total), 0) == slot_ref[...]).astype(
        jnp.float32
    ).astype(jnp.bfloat16)
    named_at = nt_dot(one_hot, named.astype(jnp.float32).astype(jnp.bfloat16))
    own_at = nt_dot(one_hot, own.astype(jnp.float32).astype(jnp.bfloat16))
    before = (
        lax.broadcasted_iota(jnp.int32, (samples, samples), 0)
        < lax.broadcasted_iota(jnp.int32, (samples, samples), 1)
    ).astype(jnp.float32).astype(jnp.bfloat16)
    rank = nn_dot(named_at.astype(jnp.bfloat16), before)
    label = label_ref[...].astype(jnp.float32) + 1.0
    own_label = own_at * label
    lane = lax.broadcasted_iota(jnp.int32, (total, LANES), 1)
    tags = jnp.zeros((total, LANES), jnp.float32)
    for r in range(MOST):
        sel = jnp.where(rank == float(r), named_at, 0.0)
        sel_bf = sel.astype(jnp.bfloat16)
        sel_ref[r] = sel_bf
        picked = nn_dot(sel_bf, normed)
        for s in range(segs):
            stage[pl.ds(segs * r + s, total, stride=rows), :] = picked[
                :, LANES * s : LANES * (s + 1)
            ]
        col = jnp.sum(sel * own_label, axis=1, keepdims=True)
        high = jnp.floor(col * (1.0 / 32.0))
        low = col - 32.0 * high
        tags = jnp.where(lane == 2 * r, high, tags)
        tags = jnp.where(lane == 2 * r + 1, low, tags)
    stage[pl.ds(MOST * segs, total, stride=rows), :] = tags
    stage[pl.ds(MOST * segs + 1, total, stride=rows), :] = jnp.zeros_like(tags)
    pay_ref[...] = stage[...].astype(jnp.bfloat16)


def centers_kernel(centers_ref, normed_ref):
    c = centers_ref[...].astype(jnp.float32)
    length = jnp.sqrt(jnp.sum(c * c, axis=1, keepdims=True) + EPSILON)
    normed_ref[...] = (c / length).astype(jnp.bfloat16)


def scores_kernel(pay_ref, normed_ref, rows_ref, cols_ref, exps_ref, stats_ref, stage):
    width = normed_ref.shape[1]
    count = normed_ref.shape[0]
    segs = width // LANES
    rows = MOST * segs + 2
    total = pay_ref.shape[0] // rows
    stage[...] = pay_ref[...].astype(jnp.float32)
    tags = stage[pl.ds(MOST * segs, total, stride=rows), :]
    lane = lax.broadcasted_iota(jnp.int32, (total, LANES), 1)
    stats = jnp.zeros((total, LANES), jnp.float32)
    normed = normed_ref[...]
    for r in range(MOST):
        part = jnp.concatenate(
            [stage[pl.ds(segs * r + s, total, stride=rows), :] for s in range(segs)], axis=1
        ).astype(jnp.bfloat16)
        rows_ref[r] = part
        col = (32.0 * tags[:, 2 * r : 2 * r + 1] + tags[:, 2 * r + 1 : 2 * r + 2] - 1.0).astype(
            jnp.int32
        )
        cols_ref[r] = jnp.broadcast_to(col, (total, LANES))
        scores = LOGIT_SCALE * nt_dot(part, normed)
        hit = lax.broadcasted_iota(jnp.int32, (total, count), 1) == col
        scores = jnp.where(hit, scores - LOGIT_SCALE * MARGIN, scores)
        exps = jnp.exp(scores)
        exps_ref[r] = exps
        stats = jnp.where(lane == r, jnp.sum(exps, axis=1, keepdims=True), stats)
        target = jnp.sum(jnp.where(hit, scores, 0.0), axis=1, keepdims=True)
        stats = jnp.where(lane == MOST + r, target, stats)
    stats_ref[...] = stats


def partial_kernel(exps_ref, cols_ref, normed_ref, sums_ref, hits_ref):
    total, count = exps_ref.shape[1:]
    normed = normed_ref[...]
    for r in range(MOST):
        hit = lax.broadcasted_iota(jnp.int32, (total, count), 1) == cols_ref[r][:, 0:1]
        sums_ref[r] = LOGIT_SCALE * nn_dot(exps_ref[r].astype(jnp.bfloat16), normed)
        hits_ref[r] = LOGIT_SCALE * nn_dot(hit.astype(jnp.float32).astype(jnp.bfloat16), normed)


def totals_kernel(stats_ref, sel_ref, gain_ref, back_ref, loss_ref):
    total = stats_ref.shape[0]
    stats = stats_ref[...]
    gain = gain_ref[...].astype(jnp.float32)
    sels = [sel_ref[r].astype(jnp.float32) for r in range(MOST)]
    denom = 0.0
    target = 0.0
    for r in range(MOST):
        denom = denom + jnp.sum(sels[r] * stats[:, r : r + 1], axis=0, keepdims=True)
        target = target + jnp.sum(
            sels[r] * stats[:, MOST + r : MOST + r + 1], axis=0, keepdims=True
        )
    loss_ref[...] = jnp.log(denom) - target
    factor = gain / denom
    lane = lax.broadcasted_iota(jnp.int32, (total, LANES), 1)
    back = jnp.zeros((total, LANES), jnp.float32)
    for r in range(MOST):
        back = jnp.where(lane == r, jnp.sum(sels[r] * factor, axis=1, keepdims=True), back)
        back = jnp.where(lane == MOST + r, jnp.sum(sels[r] * gain, axis=1, keepdims=True), back)
    back_ref[...] = back


def return_kernel(fac_ref, sums_ref, hits_ref, out_ref, stage):
    total = fac_ref.shape[0]
    width = sums_ref.shape[2]
    segs = width // LANES
    fac = fac_ref[...]
    for r in range(MOST):
        grads = fac[:, r : r + 1] * sums_ref[r] - fac[:, MOST + r : MOST + r + 1] * hits_ref[r]
        for s in range(segs):
            stage[pl.ds(segs * r + s, total, stride=MOST * segs), :] = grads[
                :, LANES * s : LANES * (s + 1)
            ]
    out_ref[...] = stage[...].astype(jnp.bfloat16)


def center_grad_kernel(fac_ref, exps_ref, cols_ref, rows_ref, centers_ref, out_ref):
    total, count = exps_ref.shape[1:]
    fac = fac_ref[...]
    unit_grad = jnp.zeros(out_ref.shape, jnp.float32)
    for r in range(MOST):
        hit = lax.broadcasted_iota(jnp.int32, (total, count), 1) == cols_ref[r][:, 0:1]
        weights = fac[:, r : r + 1] * exps_ref[r] - jnp.where(
            hit, fac[:, MOST + r : MOST + r + 1], 0.0
        )
        unit_grad = unit_grad + tn_dot(weights.astype(jnp.bfloat16), rows_ref[r])
    unit_grad = LOGIT_SCALE * unit_grad
    c = centers_ref[...].astype(jnp.float32)
    length = jnp.sqrt(jnp.sum(c * c, axis=1, keepdims=True) + EPSILON)
    unit = c / length
    along = jnp.sum(unit * unit_grad, axis=1, keepdims=True)
    out_ref[...] = ((unit_grad - unit * along) / length).astype(jnp.bfloat16)


def combine_kernel(back_ref, sel_ref, feat_ref, out_ref, stage):
    samples, width = feat_ref.shape
    total = sel_ref.shape[1]
    segs = width // LANES
    stage[...] = back_ref[...].astype(jnp.float32)
    unit_grad = jnp.zeros((samples, width), jnp.float32)
    for r in range(MOST):
        part = jnp.concatenate(
            [stage[pl.ds(segs * r + s, total, stride=MOST * segs), :] for s in range(segs)],
            axis=1,
        ).astype(jnp.bfloat16)
        unit_grad = unit_grad + tn_dot(sel_ref[r], part)
    x = feat_ref[...].astype(jnp.float32)
    norm = jnp.sqrt(jnp.sum(x * x, axis=1, keepdims=True) + EPSILON)
    unit = x / norm
    along = jnp.sum(unit * unit_grad, axis=1, keepdims=True)
    out_ref[...] = (unit_grad - unit * along) / norm


def exchange(x):
    return lax.all_to_all(x, AXES, split_axis=0, concat_axis=0, tiled=True)


def on_device(features, loss_scale, blocks, label_col, block_slot, centers):
    samples, width = features.shape
    total = block_slot.shape[0]
    count = centers.shape[0]
    segs = width // LANES
    rows = MOST * segs + 2
    bf16, f32 = jnp.bfloat16, jnp.float32
    shape = jax.ShapeDtypeStruct
    payload, sel = call(
        dispatch_kernel,
        (shape((total * rows, LANES), bf16), shape((MOST, total, samples), bf16)),
        [pltpu.VMEM((total * rows, LANES), f32)],
        "dispatch",
    )(features, blocks, label_col.reshape(1, samples), block_slot.reshape(1, total))
    payload_in = exchange(payload.reshape(total, rows // 2, 2, LANES)).reshape(total * rows, LANES)
    normed = call(centers_kernel, shape((count, width), bf16), name="normalize")(centers)
    rows_x, cols, exps, stats = call(
        scores_kernel,
        (
            shape((MOST, total, width), bf16),
            shape((MOST, total, LANES), jnp.int32),
            shape((MOST, total, count), f32),
            shape((total, LANES), f32),
        ),
        [pltpu.VMEM((total * rows, LANES), f32)],
        "scores",
    )(payload_in, normed)
    stats_in = exchange(stats.reshape(total, 1, LANES)).reshape(total, LANES)
    sums, hits = call(
        partial_kernel,
        (shape((MOST, total, width), f32), shape((MOST, total, width), f32)),
        name="partial",
    )(exps, cols, normed)
    factors, loss = call(
        totals_kernel, (shape((total, LANES), f32), shape((1, samples), f32)), name="totals"
    )(stats_in, sel, loss_scale.reshape(1, samples))
    factors_in = exchange(factors.reshape(total, 1, LANES)).reshape(total, LANES)
    returned = call(
        return_kernel,
        shape((total * MOST * segs, LANES), bf16),
        [pltpu.VMEM((total * MOST * segs, LANES), f32)],
        "returned",
    )(factors_in, sums, hits)
    back = exchange(returned.reshape(total, MOST, segs, LANES)).reshape(total * MOST * segs, LANES)
    center_grad = call(center_grad_kernel, shape((count, width), bf16), name="center_grad")(
        factors_in, exps, cols, rows_x, centers
    )
    feature_grad = call(
        combine_kernel,
        shape((samples, width), f32),
        [pltpu.VMEM((total * MOST * segs, LANES), f32)],
        "combine",
    )(back, sel, features)
    return (loss.reshape(samples), feature_grad, center_grad)


def solution(mesh):
    placed = (
        P(AXES, None),
        P(AXES),
        P(AXES, None),
        P(AXES),
        P(),
        P(AXES, None),
    )
    return jax.shard_map(
        on_device,
        mesh=mesh,
        in_specs=placed,
        out_specs=(P(AXES), P(AXES, None), P(AXES, None)),
        check_vma=False,
    )
```

profile of v0, /device:TPU:1, one launch (start us, length us, event | category | flops | bytes accessed | tf_op | source)
XLA Modules:
  0.0 205.7 jit_solution(5990172881234289887)
XLA Ops:
  0.6 1.4 copy.10.blocks_ref
  2.0 3.7 %dispatch.1 = (bf16[7168,128]{1,0:T(8,128)(2,1)}, bf16[3,512,128]{2,1,0:T(8,128)(2,1)}) custom-call(bf16[128,512]{1,0:T(8,128)(2,1)} %feat_ref.3, s32[128,8]{1,0:T(8,128)} %copy.10.blocks_ref, s32[1,128]{1,0:T(1,128)} %bitcast.26, s32[1,512]{1,0:T(1,128)} %bitcast.25), custom_call_target="tpu_custom_call" | custom-call | tf_op jit(solution)/shard_map/dispatch/pallas_call | solution.py:219
  5.7 22.1 %all-to-all-start = ((bf16[512,7,2,128]{3,2,1,0:T(2,128)(2,1)}), bf16[512,7,2,128]{3,2,1,0:T(2,128)(2,1)S(1)}, u32[]{:S(2)}, u32[]{:S(2)}) async-start(bf16[512,7,2,128]{3,2,1,0:T(2,128)(2,1)} %bitcast.21), calls=%async_computation | async-start | bytes 3670016 | tf_op jit(solution)/shard_map/all_to_all | solution.py:208
  27.9 2.7 %normalize.1.normed_ref = bf16[1024,512]{1,0:T(8,128)(2,1)} custom-call(bf16[1024,512]{1,0:T(8,128)(2,1)} %centers_ref.3), custom_call_target="tpu_custom_call" | custom-call | tf_op jit(solution)/shard_map/normalize/pallas_call | solution.py:226
  30.5 46.0 %all-to-all-done = bf16[512,7,2,128]{3,2,1,0:T(2,128)(2,1)S(1)} async-done(((bf16[512,7,2,128]{3,2,1,0:T(2,128)(2,1)}), bf16[512,7,2,128]{3,2,1,0:T(2,128)(2,1)S(1)}, u32[]{:S(2)}, u32[]{:S(2)}) %all-to-all-start) | async-done | bytes 1835040 | tf_op jit(solution)/shard_map/all_to_all | solution.py:208
  76.5 0.0 copy-start
  76.5 1.3 copy-done
  77.8 7.6 %scores.1 = (bf16[3,512,512]{2,1,0:T(8,128)(2,1)}, s32[3,512,128]{2,1,0:T(8,128)}, f32[3,512,1024]{2,1,0:T(8,128)}, f32[512,128]{1,0:T(8,128)}) custom-call(bf16[7168,128]{1,0:T(8,128)(2,1)} %bitcast.16, bf16[1024,512]{1,0:T(8,128)(2,1)} %normalize.1.normed_ref), custom_call_target="tpu_custom_call" | custom-call | tf_op jit(solution)/shard_map/scores/pallas_call | solution.py:227
  85.4 26.7 %all_to_all.20 = f32[512,1,128]{2,1,0:T(1,128)} all-to-all(f32[512,1,128]{2,1,0:T(1,128)} %bitcast.24), channel_id=1, replica_groups=mesh['dp'=128,'grp'=4] {'dp','grp'}, dimensions={0} | all-to-all | bytes 524288 | tf_op jit(solution)/shard_map/all_to_all | solution.py:208
  112.1 2.7 %totals.1 = (f32[512,128]{1,0:T(8,128)}, f32[1,128]{1,0:T(1,128)}) custom-call(f32[512,128]{1,0:T(8,128)} %bitcast.22, bf16[3,512,128]{2,1,0:T(8,128)(2,1)} %get-tuple-element.15.sel_ref, bf16[1,128]{1,0:T(2,128)(2,1)} %bitcast.27), custom_call_target="tpu_custom_call" | custom-call | tf_op jit(solution)/shard_map/totals/pallas_call | solution.py:244
  114.8 9.8 %all-to-all-start.2 = ((f32[512,1,128]{2,1,0:T(1,128)}), f32[512,1,128]{2,1,0:T(1,128)S(1)}, u32[]{:S(2)}, u32[]{:S(2)}) async-start(f32[512,1,128]{2,1,0:T(1,128)} %bitcast.23), calls=%async_computation.2 | async-start | bytes 524288 | tf_op jit(solution)/shard_map/all_to_all | solution.py:208
  124.6 8.8 %partial.1 = (f32[3,512,512]{2,1,0:T(8,128)}, f32[3,512,512]{2,1,0:T(8,128)}) custom-call(f32[3,512,1024]{2,1,0:T(8,128)} %get-tuple-element.18.exps_ref, s32[3,512,128]{2,1,0:T(8,128)} %get-tuple-element.19.cols_ref, bf16[1024,512]{1,0:T(8,128)(2,1)} %normalize.1.normed_ref), custom_call_target="tpu_custom_call" | custom-call | tf_op jit(solution)/shard_map/partial/pallas_call | solution.py:239
  133.4 7.8 %all-to-all-done.2 = f32[512,1,128]{2,1,0:T(1,128)S(1)} async-done(((f32[512,1,128]{2,1,0:T(1,128)}), f32[512,1,128]{2,1,0:T(1,128)S(1)}, u32[]{:S(2)}, u32[]{:S(2)}) %all-to-all-start.2) | async-done | bytes 262176 | tf_op jit(solution)/shard_map/all_to_all | solution.py:208
  141.1 0.0 copy-start.2
  141.1 0.7 copy-done.2
  141.8 4.9 %returned.1 = bf16[6144,128]{1,0:T(8,128)(2,1)} custom-call(f32[512,128]{1,0:T(8,128)} %bitcast.19, f32[3,512,512]{2,1,0:T(8,128)} %get-tuple-element.20.sums_ref, f32[3,512,512]{2,1,0:T(8,128)} %get-tuple-element.21.hits_ref), custom_call_target="tpu_custom_call" | custom-call | tf_op jit(solution)/shard_map/returned/pallas_call | solution.py:248
  146.7 11.7 %all-to-all-start.3 = ((bf16[512,3,4,128]{3,2,1,0:T(4,128)(2,1)}), bf16[512,3,4,128]{3,2,1,0:T(4,128)(2,1)S(1)}, u32[]{:S(2)}, u32[]{:S(2)}) async-start(bf16[512,3,4,128]{3,2,1,0:T(4,128)(2,1)} %bitcast.18), calls=%async_computation.3 | async-start | bytes 3145728 | tf_op jit(solution)/shard_map/all_to_all | solution.py:208
  158.5 7.9 %center_grad.1 = bf16[1024,512]{1,0:T(8,128)(2,1)} custom-call(f32[512,128]{1,0:T(8,128)} %bitcast.20, f32[3,512,1024]{2,1,0:T(8,128)} %get-tuple-element.18.exps_ref, s32[3,512,128]{2,1,0:T(8,128)} %get-tuple-element.19.cols_ref, bf16[3,512,512]{2,1,0:T(8,128)(2,1)} %get-tuple-element.22.rows_ref, bf16[1024,512]{1,0:T(8,128)(2,1)} %centers_ref.3), custom_call_target="tpu_custom_call" | custom-call | tf_op jit(solution)/shard_map/center_grad/pallas_call | solution.py:255
  166.4 35.2 %all-to-all-done.3 = bf16[512,3,4,128]{3,2,1,0:T(4,128)(2,1)S(1)} async-done(((bf16[512,3,4,128]{3,2,1,0:T(4,128)(2,1)}), bf16[512,3,4,128]{3,2,1,0:T(4,128)(2,1)S(1)}, u32[]{:S(2)}, u32[]{:S(2)}) %all-to-all-start.3) | async-done | bytes 1572896 | tf_op jit(solution)/shard_map/all_to_all | solution.py:208
  201.6 0.0 copy-start.1
  201.6 1.2 copy-done.1
  202.8 2.9 %combine.1 = f32[128,512]{1,0:T(8,128)} custom-call(bf16[6144,128]{1,0:T(8,128)(2,1)} %bitcast.17, bf16[3,512,128]{2,1,0:T(8,128)(2,1)} %get-tuple-element.15.sel_ref, bf16[128,512]{1,0:T(8,128)(2,1)} %feat_ref.3), custom_call_target="tpu_custom_call" | custom-call | tf_op jit(solution)/shard_map/combine/pallas_call | solution.py:258
Async XLA Ops:
  5.7 70.8 %all-to-all-start = ((bf16[512,7,2,128]{3,2,1,0:T(2,128)(2,1)}), bf16[512,7,2,128]{3,2,1,0:T(2,128)(2,1)S(1)}, u32[]{:S(2)}, u32[]{:S(2)}) async-start(bf16[512,7,2,128]{3,2,1,0:T(2,128)(2,1)} %bitcast.21), calls=%async_computation | async-start | bytes 3670016 | tf_op jit(solution)/shard_map/all_to_all | solution.py:208
  76.5 1.3 copy-start
  114.8 26.4 %all-to-all-start.2 = ((f32[512,1,128]{2,1,0:T(1,128)}), f32[512,1,128]{2,1,0:T(1,128)S(1)}, u32[]{:S(2)}, u32[]{:S(2)}) async-start(f32[512,1,128]{2,1,0:T(1,128)} %bitcast.23), calls=%async_computation.2 | async-start | bytes 524288 | tf_op jit(solution)/shard_map/all_to_all | solution.py:208
  141.1 0.7 copy-start.2
  146.7 54.9 %all-to-all-start.3 = ((bf16[512,3,4,128]{3,2,1,0:T(4,128)(2,1)}), bf16[512,3,4,128]{3,2,1,0:T(4,128)(2,1)S(1)}, u32[]{:S(2)}, u32[]{:S(2)}) async-start(bf16[512,3,4,128]{3,2,1,0:T(4,128)(2,1)} %bitcast.18), calls=%async_computation.3 | async-start | bytes 3145728 | tf_op jit(solution)/shard_map/all_to_all | solution.py:208
  201.6 1.2 copy-start.1
where the time goes:
time: 206 us
  waiting for transfers between devices  89 us (43%)
  starting transfers between devices  43.7 us (21%)
  Pallas kernels  41.1 us (20%)
  blocking collectives  26.7 us (13%)
  local copies, waits for them, and re-layouts  4.54 us (2%)
    all_to_all x3, waiting for transfers between devices, exchange(): return lax.all_to_all(x, AXES, split_axis=0, concat_axis=0, tiled=True)  89 us
    all_to_all x3, starting transfers between devices, exchange(): return lax.all_to_all(x, AXES, split_axis=0, concat_axis=0, tiled=True)  43.7 us
    all_to_all x1, blocking collectives, exchange(): return lax.all_to_all(x, AXES, split_axis=0, concat_axis=0, tiled=True)  26.7 us
    pallas_call x1, Pallas kernels, on_device(): call(partial_kernel, (shape((MOST, total, width), f32), shape((MOST, tota...  8.78 us
    pallas_call x1, Pallas kernels, on_device(): call(center_grad_kernel, shape((count, width), bf16), name='center_grad')  7.91 us
    pallas_call x1, Pallas kernels, on_device(): call(scores_kernel, (shape((MOST, total, width), bf16), shape((MOST, tota...  7.61 us
    pallas_call x1, Pallas kernels, on_device(): call(return_kernel, shape((total * MOST * segs, LANES), bf16), [pltpu.VME...  4.89 us
    unnamed x7, local copies, waits for them, and re-layouts  4.54 us
  transfers between devices with their start and end apart: 3, of which 3 were waited for; matrix products, arithmetic and copies ran while one was open for 0% of the time, Pallas kernels for 9%

commit v1 on v0

v1 whole, which is shorter than its diff:
```python
import jax
import jax.numpy as jnp
from jax import lax
from jax.experimental import pallas as pl
from jax.experimental.pallas import tpu as pltpu
from jax.sharding import PartitionSpec as P

BLOCK = 1024
MOST = 3
LANES = 128
MARGIN = 0.35
LOGIT_SCALE = 64.0
EPSILON = 1e-06
AXES = ("dp", "grp")

MIB = 1024 * 1024


def nt_dot(a, b):
    return lax.dot_general(a, b, (((1,), (1,)), ((), ())), preferred_element_type=jnp.float32)


def tn_dot(a, b):
    return lax.dot_general(a, b, (((0,), (0,)), ((), ())), preferred_element_type=jnp.float32)


def nn_dot(a, b):
    return jnp.dot(a, b, preferred_element_type=jnp.float32)


WHOLE = pl.BlockSpec(memory_space=pltpu.VMEM)


def block(shape, place):
    return pl.BlockSpec(shape, place)


def call(name, kernel, args, outs, scratch=(), grid=(), ins=None, to=None, limit=28):
    return pl.pallas_call(
        kernel,
        out_shape=tuple(outs),
        grid=grid,
        in_specs=ins or [WHOLE] * len(args),
        out_specs=to or tuple(WHOLE for _ in outs),
        scratch_shapes=list(scratch),
        compiler_params=pltpu.CompilerParams(vmem_limit_bytes=limit * MIB),
        name=name,
    )(*args)


def near(x):
    return pltpu.with_memory_space_constraint(x, pltpu.VMEM)


def away(x):
    return pltpu.with_memory_space_constraint(x, pltpu.HBM)


def dispatch_kernel(feat_ref, blocks_ref, label_ref, slot_ref, pay_ref, sel_ref, stage):
    samples, width = feat_ref.shape
    total = slot_ref.shape[1]
    segs = width // LANES
    rows = MOST * segs + 2
    x = feat_ref[...].astype(jnp.float32)
    norm = jnp.sqrt(jnp.sum(x * x, axis=1, keepdims=True) + EPSILON)
    normed = (x / norm).astype(jnp.bfloat16)
    named_by = blocks_ref[...]
    block_iota = lax.broadcasted_iota(jnp.int32, (total, samples), 0)
    own = block_iota == named_by[0:1]
    named = own
    for k in range(1, blocks_ref.shape[0]):
        named = named | (block_iota == named_by[k : k + 1])
    both = jnp.concatenate([named.astype(jnp.float32), own.astype(jnp.float32)], axis=1)
    one_hot = (lax.broadcasted_iota(jnp.int32, (total, total), 0) == slot_ref[...]).astype(
        jnp.float32
    ).astype(jnp.bfloat16)
    both_at = nn_dot(one_hot, both.astype(jnp.bfloat16))
    named_at = both_at[:, :samples]
    own_at = both_at[:, samples:]
    before = (
        lax.broadcasted_iota(jnp.int32, (samples, samples), 0)
        < lax.broadcasted_iota(jnp.int32, (samples, samples), 1)
    ).astype(jnp.float32).astype(jnp.bfloat16)
    rank = nn_dot(named_at.astype(jnp.bfloat16), before)
    label = label_ref[...].astype(jnp.float32) + 1.0
    own_label = own_at * label
    lane = lax.broadcasted_iota(jnp.int32, (total, LANES), 1)
    tags = jnp.zeros((total, LANES), jnp.float32)
    for r in range(MOST):
        sel = jnp.where(rank == float(r), named_at, 0.0)
        sel_bf = sel.astype(jnp.bfloat16)
        sel_ref[r] = sel_bf
        picked = nn_dot(sel_bf, normed)
        for s in range(segs):
            stage[pl.ds(segs * r + s, total, stride=rows), :] = picked[
                :, LANES * s : LANES * (s + 1)
            ]
        col = jnp.sum(sel * own_label, axis=1, keepdims=True)
        high = jnp.floor(col * (1.0 / 32.0))
        low = col - 32.0 * high
        tags = jnp.where(lane == 2 * r, high, tags)
        tags = jnp.where(lane == 2 * r + 1, low, tags)
    stage[pl.ds(MOST * segs, total, stride=rows), :] = tags
    stage[pl.ds(MOST * segs + 1, total, stride=rows), :] = jnp.zeros_like(tags)
    pay_ref[...] = stage[...].astype(jnp.bfloat16)


def centers_kernel(centers_ref, scaled_ref, across_ref):
    c = centers_ref[...].astype(jnp.float32)
    length = jnp.sqrt(jnp.sum(c * c, axis=1, keepdims=True) + EPSILON)
    scaled = LOGIT_SCALE * (c / length).astype(jnp.bfloat16).astype(jnp.float32)
    scaled_ref[...] = scaled.astype(jnp.bfloat16)
    across_ref[...] = scaled.T.astype(jnp.bfloat16)


def scores_kernel(pay_ref, across_ref, rows_ref, exps_ref, cols_ref, stats_ref, stage):
    width, count = across_ref.shape
    segs = width // LANES
    rows = MOST * segs + 2
    total = pay_ref.shape[0] // rows
    r = pl.program_id(0)

    @pl.when(r == 0)
    def _():
        stage[...] = pay_ref[...].astype(jnp.float32)
        cols_ref[...] = jnp.zeros_like(cols_ref)
        stats_ref[...] = jnp.zeros_like(stats_ref)

    lane = lax.broadcasted_iota(jnp.int32, (total, LANES), 1)
    tags = stage[pl.ds(MOST * segs, total, stride=rows), :]
    shares = jnp.where(lane == 2 * r, 32.0, 0.0) + jnp.where(lane == 2 * r + 1, 1.0, 0.0)
    col = jnp.sum(tags * shares, axis=1, keepdims=True).astype(jnp.int32) - 1
    part = jnp.concatenate(
        [stage[pl.ds(segs * r + s, total, stride=rows), :] for s in range(segs)], axis=1
    ).astype(jnp.bfloat16)
    rows_ref[0] = part
    scores = nn_dot(part, across_ref[...])
    hit = lax.broadcasted_iota(jnp.int32, (total, count), 1) == col
    scores = jnp.where(hit, scores - LOGIT_SCALE * MARGIN, scores)
    exps = jnp.exp(scores)
    exps_ref[0] = exps
    sums = jnp.sum(exps, axis=1, keepdims=True)
    target = jnp.sum(jnp.where(hit, scores, 0.0), axis=1, keepdims=True)
    stats = jnp.where(lane == r, sums, stats_ref[...])
    stats_ref[...] = jnp.where(lane == MOST + r, target, stats)
    cols_ref[...] = jnp.where(lane == r, col, cols_ref[...])


def partial_kernel(exps_ref, cols_ref, scaled_ref, sums_ref, hits_ref):
    total, count = exps_ref.shape[1:]
    r = pl.program_id(0)
    lane = lax.broadcasted_iota(jnp.int32, (total, LANES), 1)
    col = jnp.sum(jnp.where(lane == r, cols_ref[...], 0), axis=1, keepdims=True)
    hit = lax.broadcasted_iota(jnp.int32, (total, count), 1) == col
    exps = jnp.where(hit, 0.0, exps_ref[0]).astype(jnp.bfloat16)
    sums_ref[0] = nn_dot(exps, scaled_ref[...])
    chosen = jnp.where(hit, 1.0, 0.0).astype(jnp.bfloat16)
    hits_ref[0] = nn_dot(chosen, scaled_ref[...]).astype(jnp.bfloat16)


def totals_kernel(stats_ref, sel_ref, gain_ref, back_ref, loss_ref):
    total = stats_ref.shape[0]
    stats = stats_ref[...]
    gain = gain_ref[...].astype(jnp.float32)
    sels = [sel_ref[r].astype(jnp.float32) for r in range(MOST)]
    denom = 0.0
    target = 0.0
    for r in range(MOST):
        denom = denom + jnp.sum(sels[r] * stats[:, r : r + 1], axis=0, keepdims=True)
        target = target + jnp.sum(
            sels[r] * stats[:, MOST + r : MOST + r + 1], axis=0, keepdims=True
        )
    loss_ref[...] = jnp.log(denom) - target
    factor = gain / denom
    lane = lax.broadcasted_iota(jnp.int32, (total, LANES), 1)
    back = jnp.zeros((total, LANES), jnp.float32)
    for r in range(MOST):
        back = jnp.where(lane == r, jnp.sum(sels[r] * factor, axis=1, keepdims=True), back)
        back = jnp.where(lane == MOST + r, jnp.sum(sels[r] * gain, axis=1, keepdims=True), back)
    back_ref[...] = back


def return_kernel(fac_ref, stats_ref, sums_ref, hits_ref, out_ref, stage):
    some, width = sums_ref.shape[1:]
    segs = width // LANES
    fac = fac_ref[pl.ds(pl.multiple_of(pl.program_id(0) * some, some), some), :]
    stats = stats_ref[...]
    for r in range(MOST):
        factor = fac[:, r : r + 1]
        at_label = factor * jnp.exp(stats[:, MOST + r : MOST + r + 1])
        at_label = at_label - fac[:, MOST + r : MOST + r + 1]
        grads = factor * sums_ref[r] + at_label * hits_ref[r].astype(jnp.float32)
        for s in range(segs):
            stage[pl.ds(segs * r + s, some, stride=MOST * segs), :] = grads[
                :, LANES * s : LANES * (s + 1)
            ]
    out_ref[...] = stage[...].astype(jnp.bfloat16)


def center_grad_kernel(fac_ref, exps_ref, cols_ref, rows_ref, centers_ref, out_ref):
    total, count = exps_ref.shape[1:]
    fac = fac_ref[...]
    cols = cols_ref[...]
    unit_grad = jnp.zeros(out_ref.shape, jnp.float32)
    for r in range(MOST):
        hit = lax.broadcasted_iota(jnp.int32, (total, count), 1) == cols[:, r : r + 1]
        weights = fac[:, r : r + 1] * exps_ref[r] - jnp.where(
            hit, fac[:, MOST + r : MOST + r + 1], 0.0
        )
        unit_grad = unit_grad + tn_dot(weights.astype(jnp.bfloat16), rows_ref[r])
    unit_grad = LOGIT_SCALE * unit_grad
    c = centers_ref[...].astype(jnp.float32)
    length = jnp.sqrt(jnp.sum(c * c, axis=1, keepdims=True) + EPSILON)
    unit = c / length
    along = jnp.sum(unit * unit_grad, axis=1, keepdims=True)
    out_ref[...] = ((unit_grad - unit * along) / length).astype(jnp.bfloat16)


def combine_kernel(back_ref, sel_ref, feat_ref, out_ref, stage):
    samples, width = feat_ref.shape
    total = sel_ref.shape[1]
    segs = width // LANES
    stage[...] = back_ref[...].astype(jnp.float32)
    unit_grad = jnp.zeros((samples, width), jnp.float32)
    for r in range(MOST):
        part = jnp.concatenate(
            [stage[pl.ds(segs * r + s, total, stride=MOST * segs), :] for s in range(segs)],
            axis=1,
        ).astype(jnp.bfloat16)
        unit_grad = unit_grad + tn_dot(sel_ref[r], part)
    x = feat_ref[...].astype(jnp.float32)
    norm = jnp.sqrt(jnp.sum(x * x, axis=1, keepdims=True) + EPSILON)
    unit = x / norm
    along = jnp.sum(unit * unit_grad, axis=1, keepdims=True)
    out_ref[...] = (unit_grad - unit * along) / norm


def exchange(x):
    return lax.all_to_all(x, AXES, split_axis=0, concat_axis=0, tiled=True)


def on_device(features, loss_scale, blocks, label_col, block_slot, centers):
    samples, width = features.shape
    total = block_slot.shape[0]
    count = centers.shape[0]
    segs = width // LANES
    rows = MOST * segs + 2
    back_rows = MOST * segs
    bf16, f32 = jnp.bfloat16, jnp.float32
    far, here = pltpu.HBM, pltpu.VMEM
    chunks = 4
    some = total // chunks
    payload, sel = call(
        "dispatch",
        dispatch_kernel,
        tuple(
            away(x)
            for x in (
                features,
                blocks.T,
                label_col.reshape(1, samples),
                block_slot.reshape(1, total),
            )
        ),
        (far((total * rows, LANES), bf16), far((MOST, total, samples), bf16)),
        [here((total * rows, LANES), f32)],
    )
    payload_in = exchange(payload.reshape(total, rows // 2, 2, LANES)).reshape(total * rows, LANES)
    scaled, across = call(
        "normalize",
        centers_kernel,
        (centers,),
        (far((count, width), bf16), far((width, count), bf16)),
    )
    rows_x, exps, cols, stats = call(
        "scores",
        scores_kernel,
        (near(payload_in), away(across)),
        (
            far((MOST, total, width), bf16),
            far((MOST, total, count), f32),
            far((total, LANES), jnp.int32),
            far((total, LANES), f32),
        ),
        [here((total * rows, LANES), f32)],
        grid=(MOST,),
        to=(
            block((1, total, width), lambda r: (r, 0, 0)),
            block((1, total, count), lambda r: (r, 0, 0)),
            block((total, LANES), lambda r: (0, 0)),
            block((total, LANES), lambda r: (0, 0)),
        ),
    )
    stats_in = exchange(stats.reshape(total, 1, LANES)).reshape(total, LANES)
    sums, hits = call(
        "partial",
        partial_kernel,
        (away(exps), away(cols), away(scaled)),
        (far((MOST, total, width), f32), far((MOST, total, width), bf16)),
        grid=(MOST,),
        ins=[block((1, total, count), lambda r: (r, 0, 0)), WHOLE, WHOLE],
        to=(
            block((1, total, width), lambda r: (r, 0, 0)),
            block((1, total, width), lambda r: (r, 0, 0)),
        ),
    )
    factors, loss = call(
        "totals",
        totals_kernel,
        (near(stats_in), near(sel), loss_scale.reshape(1, samples)),
        (far((total, LANES), f32), far((1, samples), f32)),
    )
    factors_in = exchange(factors.reshape(total, 1, LANES)).reshape(total, LANES)
    (returned,) = call(
        "returned",
        return_kernel,
        (near(factors_in), away(stats), away(sums), away(hits)),
        (far((total * back_rows, LANES), bf16),),
        [here((some * back_rows, LANES), f32)],
        grid=(chunks,),
        ins=[
            WHOLE,
            block((some, LANES), lambda d: (d, 0)),
            block((MOST, some, width), lambda d: (0, d, 0)),
            block((MOST, some, width), lambda d: (0, d, 0)),
        ],
        to=(block((some * back_rows, LANES), lambda d: (d, 0)),),
    )
    back = exchange(returned.reshape(total, MOST, segs, LANES)).reshape(total * back_rows, LANES)
    (center_grad,) = call(
        "center_grad",
        center_grad_kernel,
        (near(factors_in), away(exps), away(cols), away(rows_x), away(centers)),
        (far((count, width), bf16),),
    )
    (feature_grad,) = call(
        "combine",
        combine_kernel,
        (near(back), near(sel), away(features)),
        (far((samples, width), f32),),
        [here((total * back_rows, LANES), f32)],
    )
    return (loss.reshape(samples), feature_grad, center_grad)


def solution(mesh):
    placed = (
        P(AXES, None),
        P(AXES),
        P(AXES, None),
        P(AXES),
        P(),
        P(AXES, None),
    )
    return jax.shard_map(
        on_device,
        mesh=mesh,
        in_specs=placed,
        out_specs=(P(AXES), P(AXES, None), P(AXES, None)),
        check_vma=False,
    )
```

time: 206 us -> 197 us (0.956)
  Pallas kernels: 41.1 us -> 35.8 us
  local copies, waits for them, and re-layouts: 4.54 us -> 0.01 us
  waiting for transfers between devices: 89 us -> 91.3 us
    pallas_call x8, Pallas kernels: 41.1 us -> 35.8 us  [call(): pl.pallas_call(kernel, out_shape=tuple(outs), grid=grid, in_specs=ins or...]
    unnamed x7 -> x6, local copies, waits for them, and re-layouts: 4.54 us -> 0.01 us
    all_to_all x3, waiting for transfers between devices: 89 us -> 91.3 us  [exchange(): return lax.all_to_all(x, AXES, split_axis=0, concat_axis=0, tiled=True)]
where the time goes in v1:
time: 197 us; the launch traced here: 196 us
  waiting for transfers between devices  91.3 us (46%)
  starting transfers between devices  42.1 us (21%)
  Pallas kernels  35.8 us (18%)
  blocking collectives  26.2 us (13%)
    all_to_all x3, waiting for transfers between devices, exchange(): return lax.all_to_all(x, AXES, split_axis=0, concat_axis=0, tiled=True)  91.3 us
    all_to_all x3, starting transfers between devices, exchange(): return lax.all_to_all(x, AXES, split_axis=0, concat_axis=0, tiled=True)  42.1 us
    pallas_call x8, Pallas kernels, call(): pl.pallas_call(kernel, out_shape=tuple(outs), grid=grid, in_specs=ins or...  35.8 us
    all_to_all x1, blocking collectives, exchange(): return lax.all_to_all(x, AXES, split_axis=0, concat_axis=0, tiled=True)  26.2 us
  transfers between devices with their start and end apart: 3, of which 3 were waited for; matrix products, arithmetic and copies ran while one was open for 0% of the time, Pallas kernels for 9%

profile of v1, /device:TPU:1, one launch (start us, length us, event | category | flops | bytes accessed | tf_op | source)
XLA Modules:
  0.0 196.0 jit_solution(4314415799185279813)
XLA Ops:
  0.6 3.6 %dispatch.1 = (bf16[7168,128]{1,0:T(8,128)(2,1)}, bf16[3,512,128]{2,1,0:T(8,128)(2,1)}) custom-call(bf16[128,512]{1,0:T(8,128)(2,1)} %feat_ref.3, s32[8,128]{1,0:T(8,128)} %bitcast.27, s32[1,128]{1,0:T(1,128)} %bitcast.29, s32[1,512]{1,0:T(1,128)} %bitcast.28), custom_call_target="tpu_custom_call" | custom-call | tf_op jit(solution)/shard_map/dispatch/pallas_call | solution.py:39
  4.2 0.0 copy-start
  4.2 22.1 %all-to-all-start = ((bf16[512,7,2,128]{3,2,1,0:T(2,128)(2,1)}), bf16[512,7,2,128]{3,2,1,0:T(2,128)(2,1)S(1)}, u32[]{:S(2)}, u32[]{:S(2)}) async-start(bf16[512,7,2,128]{3,2,1,0:T(2,128)(2,1)} %bitcast.24), calls=%async_computation | async-start | bytes 3670016 | tf_op jit(solution)/shard_map/all_to_all | solution.py:239
  26.3 0.0 copy-done
  26.4 2.2 %normalize.1 = (bf16[1024,512]{1,0:T(8,128)(2,1)}, bf16[512,1024]{1,0:T(8,128)(2,1)}) custom-call(bf16[1024,512]{1,0:T(8,128)(2,1)S(1)} %copy-done), custom_call_target="tpu_custom_call" | custom-call | tf_op jit(solution)/shard_map/normalize/pallas_call | solution.py:39
  28.5 0.0 copy-start.1
  28.5 0.0 copy-start.2
  28.5 46.5 %all-to-all-done = bf16[512,7,2,128]{3,2,1,0:T(2,128)(2,1)S(1)} async-done(((bf16[512,7,2,128]{3,2,1,0:T(2,128)(2,1)}), bf16[512,7,2,128]{3,2,1,0:T(2,128)(2,1)S(1)}, u32[]{:S(2)}, u32[]{:S(2)}) %all-to-all-start) | async-done | bytes 1835040 | tf_op jit(solution)/shard_map/all_to_all | solution.py:239
  75.0 6.5 %scores.1 = (bf16[3,512,512]{2,1,0:T(8,128)(2,1)}, f32[3,512,1024]{2,1,0:T(8,128)}, s32[512,128]{1,0:T(8,128)}, f32[512,128]{1,0:T(8,128)}) custom-call(bf16[7168,128]{1,0:T(8,128)(2,1)S(1)} %bitcast.17, bf16[512,1024]{1,0:T(8,128)(2,1)} %get-tuple-element.16.across_ref), custom_call_target="tpu_custom_call" | custom-call | tf_op jit(solution)/shard_map/scores/pallas_call | solution.py:39
  81.5 26.2 %all_to_all.20 = f32[512,1,128]{2,1,0:T(1,128)S(1)} all-to-all(f32[512,1,128]{2,1,0:T(1,128)} %bitcast.25), channel_id=1, replica_groups=mesh['dp'=128,'grp'=4] {'dp','grp'}, dimensions={0} | all-to-all | bytes 524288 | tf_op jit(solution)/shard_map/all_to_all | solution.py:239
  107.8 0.0 copy-done.1
  107.8 0.0 copy-done.2
  107.8 1.6 totals.1
  109.4 9.8 %all-to-all-start.2 = ((f32[512,1,128]{2,1,0:T(1,128)}), f32[512,1,128]{2,1,0:T(1,128)S(1)}, u32[]{:S(2)}, u32[]{:S(2)}) async-start(f32[512,1,128]{2,1,0:T(1,128)} %bitcast.26), calls=%async_computation.2 | async-start | bytes 524288 | tf_op jit(solution)/shard_map/all_to_all | solution.py:239
  119.2 7.2 %partial.1 = (f32[3,512,512]{2,1,0:T(8,128)}, bf16[3,512,512]{2,1,0:T(8,128)(2,1)}) custom-call(f32[3,512,1024]{2,1,0:T(8,128)} %get-tuple-element.21.exps_ref, s32[512,128]{1,0:T(8,128)} %get-tuple-element.22.cols_ref, bf16[1024,512]{1,0:T(8,128)(2,1)} %get-tuple-element.23.scaled_ref), custom_call_target="tpu_custom_call" | custom-call | tf_op jit(solution)/shard_map/partial/pallas_call | solution.py:39
  126.4 9.4 %all-to-all-done.2 = f32[512,1,128]{2,1,0:T(1,128)S(1)} async-done(((f32[512,1,128]{2,1,0:T(1,128)}), f32[512,1,128]{2,1,0:T(1,128)S(1)}, u32[]{:S(2)}, u32[]{:S(2)}) %all-to-all-start.2) | async-done | bytes 262176 | tf_op jit(solution)/shard_map/all_to_all | solution.py:239
  135.8 4.7 %returned.1 = bf16[6144,128]{1,0:T(8,128)(2,1)} custom-call(f32[512,128]{1,0:T(8,128)S(1)} %bitcast.19, f32[512,128]{1,0:T(8,128)} %get-tuple-element.17.stats_ref, f32[3,512,512]{2,1,0:T(8,128)} %get-tuple-element.24.sums_ref, bf16[3,512,512]{2,1,0:T(8,128)(2,1)} %get-tuple-element.25.hits_ref), custom_call_target="tpu_custom_call" | custom-call | tf_op jit(solution)/shard_map/returned/pallas_call | solution.py:39
  140.5 10.2 %all-to-all-start.3 = ((bf16[512,3,4,128]{3,2,1,0:T(4,128)(2,1)}), bf16[512,3,4,128]{3,2,1,0:T(4,128)(2,1)S(1)}, u32[]{:S(2)}, u32[]{:S(2)}) async-start(bf16[512,3,4,128]{3,2,1,0:T(4,128)(2,1)} %bitcast.23), calls=%async_computation.3 | async-start | bytes 3145728 | tf_op jit(solution)/shard_map/all_to_all | solution.py:239
  150.7 7.7 %center_grad.1 = bf16[1024,512]{1,0:T(8,128)(2,1)} custom-call(f32[512,128]{1,0:T(8,128)S(1)} %bitcast.20, f32[3,512,1024]{2,1,0:T(8,128)} %get-tuple-element.21.exps_ref, s32[512,128]{1,0:T(8,128)} %get-tuple-element.22.cols_ref, bf16[3,512,512]{2,1,0:T(8,128)(2,1)} %get-tuple-element.26.rows_ref, bf16[1024,512]{1,0:T(8,128)(2,1)} %centers_ref.3), custom_call_target="tpu_custom_call" | custom-call | tf_op jit(solution)/shard_map/center_grad/pallas_call | solution.py:39
  158.4 35.4 %all-to-all-done.3 = bf16[512,3,4,128]{3,2,1,0:T(4,128)(2,1)S(1)} async-done(((bf16[512,3,4,128]{3,2,1,0:T(4,128)(2,1)}), bf16[512,3,4,128]{3,2,1,0:T(4,128)(2,1)S(1)}, u32[]{:S(2)}, u32[]{:S(2)}) %all-to-all-start.3) | async-done | bytes 1572896 | tf_op jit(solution)/shard_map/all_to_all | solution.py:239
  193.8 2.3 %combine.1 = f32[128,512]{1,0:T(8,128)} custom-call(bf16[6144,128]{1,0:T(8,128)(2,1)S(1)} %bitcast.18, bf16[3,512,128]{2,1,0:T(8,128)(2,1)S(1)} %copy-done.1, bf16[128,512]{1,0:T(8,128)(2,1)} %feat_ref.3), custom_call_target="tpu_custom_call" | custom-call | tf_op jit(solution)/shard_map/combine/pallas_call | solution.py:39
Async XLA Ops:
  4.2 22.2 %copy-start = (bf16[1024,512]{1,0:T(8,128)(2,1)S(1)}, bf16[1024,512]{1,0:T(8,128)(2,1)}, u32[]{:S(2)}) copy-start(bf16[1024,512]{1,0:T(8,128)(2,1)} %centers_ref.3) | copy-start | bytes 3145732
  4.2 70.8 %all-to-all-start = ((bf16[512,7,2,128]{3,2,1,0:T(2,128)(2,1)}), bf16[512,7,2,128]{3,2,1,0:T(2,128)(2,1)S(1)}, u32[]{:S(2)}, u32[]{:S(2)}) async-start(bf16[512,7,2,128]{3,2,1,0:T(2,128)(2,1)} %bitcast.24), calls=%async_computation | async-start | bytes 3670016 | tf_op jit(solution)/shard_map/all_to_all | solution.py:239
  28.5 79.3 %copy-start.1 = (bf16[3,512,128]{2,1,0:T(8,128)(2,1)S(1)}, bf16[3,512,128]{2,1,0:T(8,128)(2,1)}, u32[]{:S(2)}) copy-start(bf16[3,512,128]{2,1,0:T(8,128)(2,1)} %get-tuple-element.18.sel_ref) | copy-start | bytes 1179652
  28.5 79.3 %copy-start.2 = (bf16[128]{0:T(256)(128)(2,1)S(1)}, bf16[128]{0:T(256)(128)(2,1)}, u32[]{:S(2)}) copy-start(bf16[128]{0:T(256)(128)(2,1)} %param.7) | copy-start | bytes 772
  109.4 26.4 %all-to-all-start.2 = ((f32[512,1,128]{2,1,0:T(1,128)}), f32[512,1,128]{2,1,0:T(1,128)S(1)}, u32[]{:S(2)}, u32[]{:S(2)}) async-start(f32[512,1,128]{2,1,0:T(1,128)} %bitcast.26), calls=%async_computation.2 | async-start | bytes 524288 | tf_op jit(solution)/shard_map/all_to_all | solution.py:239
  140.5 53.3 %all-to-all-start.3 = ((bf16[512,3,4,128]{3,2,1,0:T(4,128)(2,1)}), bf16[512,3,4,128]{3,2,1,0:T(4,128)(2,1)S(1)}, u32[]{:S(2)}, u32[]{:S(2)}) async-start(bf16[512,3,4,128]{3,2,1,0:T(4,128)(2,1)} %bitcast.23), calls=%async_computation.3 | async-start | bytes 3145728 | tf_op jit(solution)/shard_map/all_to_all | solution.py:239

commit v2 on v1

--- a/solution.py
+++ b/solution.py
@@ -1,8 +1,11 @@
+import functools
+
 import jax
 import jax.numpy as jnp
 from jax import lax
 from jax.experimental import pallas as pl
 from jax.experimental.pallas import tpu as pltpu
+from jax.sharding import Mesh
 from jax.sharding import PartitionSpec as P
 
 BLOCK = 1024
@@ -11,7 +14,8 @@
 MARGIN = 0.35
 LOGIT_SCALE = 64.0
 EPSILON = 1e-06
-AXES = ("dp", "grp")
+AXES = ("z", "y", "core", "grp")
+PLANE = ("y", "core", "grp")
 
 MIB = 1024 * 1024
 
@@ -56,7 +60,9 @@
     return pltpu.with_memory_space_constraint(x, pltpu.HBM)
 
 
-def dispatch_kernel(feat_ref, blocks_ref, label_ref, slot_ref, pay_ref, sel_ref, stage):
+def dispatch_kernel(
+    feat_ref, blocks_ref, label_ref, gain_ref, slot_ref, pay_ref, sel_ref, stage
+):
     samples, width = feat_ref.shape
     total = slot_ref.shape[1]
     segs = width // LANES
@@ -83,8 +89,11 @@
     ).astype(jnp.float32).astype(jnp.bfloat16)
     rank = nn_dot(named_at.astype(jnp.bfloat16), before)
     label = label_ref[...].astype(jnp.float32) + 1.0
-    own_label = own_at * label
-    lane = lax.broadcasted_iota(jnp.int32, (total, LANES), 1)
+    high = jnp.floor(label * (1.0 / 32.0))
+    low = label - 32.0 * high
+    gain = gain_ref[...].astype(jnp.float32)
+    field = lax.broadcasted_iota(jnp.int32, (LANES, samples), 0)
+    ids = lax.broadcasted_iota(jnp.int32, (LANES, samples), 1).astype(jnp.float32) + 1.0
     tags = jnp.zeros((total, LANES), jnp.float32)
     for r in range(MOST):
         sel = jnp.where(rank == float(r), named_at, 0.0)
@@ -95,11 +104,10 @@
             stage[pl.ds(segs * r + s, total, stride=rows), :] = picked[
                 :, LANES * s : LANES * (s + 1)
             ]
-        col = jnp.sum(sel * own_label, axis=1, keepdims=True)
-        high = jnp.floor(col * (1.0 / 32.0))
-        low = col - 32.0 * high
-        tags = jnp.where(lane == 2 * r, high, tags)
-        tags = jnp.where(lane == 2 * r + 1, low, tags)
+        own_tags = jnp.where(field == 4 * r, high, jnp.where(field == 4 * r + 1, low, 0.0))
+        all_tags = jnp.where(field == 4 * r + 2, ids, jnp.where(field == 4 * r + 3, gain, 0.0))
+        tags = tags + nt_dot((sel * own_at).astype(jnp.bfloat16), own_tags.astype(jnp.bfloat16))
+        tags = tags + nt_dot(sel_bf, all_tags.astype(jnp.bfloat16))
     stage[pl.ds(MOST * segs, total, stride=rows), :] = tags
     stage[pl.ds(MOST * segs + 1, total, stride=rows), :] = jnp.zeros_like(tags)
     pay_ref[...] = stage[...].astype(jnp.bfloat16)
@@ -113,23 +121,24 @@
     across_ref[...] = scaled.T.astype(jnp.bfloat16)
 
 
-def scores_kernel(pay_ref, across_ref, rows_ref, exps_ref, cols_ref, stats_ref, stage):
+def scores_kernel(pay_ref, across_ref, rows_ref, exps_ref, tags_ref, stats_ref, brief_ref, stage):
     width, count = across_ref.shape
     segs = width // LANES
     rows = MOST * segs + 2
     total = pay_ref.shape[0] // rows
+    peers = brief_ref.shape[0]
+    span = LANES * peers // total
     r = pl.program_id(0)
 
     @pl.when(r == 0)
     def _():
         stage[...] = pay_ref[...].astype(jnp.float32)
-        cols_ref[...] = jnp.zeros_like(cols_ref)
+        tags_ref[...] = stage[pl.ds(MOST * segs, total, stride=rows), :]
         stats_ref[...] = jnp.zeros_like(stats_ref)
 
     lane = lax.broadcasted_iota(jnp.int32, (total, LANES), 1)
-    tags = stage[pl.ds(MOST * segs, total, stride=rows), :]
-    shares = jnp.where(lane == 2 * r, 32.0, 0.0) + jnp.where(lane == 2 * r + 1, 1.0, 0.0)
-    col = jnp.sum(tags * shares, axis=1, keepdims=True).astype(jnp.int32) - 1
+    shares = jnp.where(lane == 4 * r, 32.0, 0.0) + jnp.where(lane == 4 * r + 1, 1.0, 0.0)
+    col = jnp.sum(tags_ref[...] * shares, axis=1, keepdims=True).astype(jnp.int32) - 1
     part = jnp.concatenate(
         [stage[pl.ds(segs * r + s, total, stride=rows), :] for s in range(segs)], axis=1
     ).astype(jnp.bfloat16)
@@ -143,14 +152,25 @@
     target = jnp.sum(jnp.where(hit, scores, 0.0), axis=1, keepdims=True)
     stats = jnp.where(lane == r, sums, stats_ref[...])
     stats_ref[...] = jnp.where(lane == MOST + r, target, stats)
-    cols_ref[...] = jnp.where(lane == r, col, cols_ref[...])
-
-
-def partial_kernel(exps_ref, cols_ref, scaled_ref, sums_ref, hits_ref):
+
+    @pl.when(r == MOST - 1)
+    def _():
+        stats = stats_ref[...]
+        for k in range(MOST):
+            ids = tags_ref[:, 4 * k + 2 : 4 * k + 3] - 1.0
+            stats = jnp.where(lane == 2 * MOST + k, ids, stats)
+        brief = stats[:peers]
+        for j in range(1, total // peers):
+            brief = brief + pltpu.roll(stats[peers * j : peers * (j + 1)], span * j, 1)
+        brief_ref[...] = brief
+
+
+def partial_kernel(exps_ref, tags_ref, scaled_ref, sums_ref, hits_ref):
     total, count = exps_ref.shape[1:]
     r = pl.program_id(0)
     lane = lax.broadcasted_iota(jnp.int32, (total, LANES), 1)
-    col = jnp.sum(jnp.where(lane == r, cols_ref[...], 0), axis=1, keepdims=True)
+    shares = jnp.where(lane == 4 * r, 32.0, 0.0) + jnp.where(lane == 4 * r + 1, 1.0, 0.0)
+    col = jnp.sum(tags_ref[...] * shares, axis=1, keepdims=True).astype(jnp.int32) - 1
     hit = lax.broadcasted_iota(jnp.int32, (total, count), 1) == col
     exps = jnp.where(hit, 0.0, exps_ref[0]).astype(jnp.bfloat16)
     sums_ref[0] = nn_dot(exps, scaled_ref[...])
@@ -158,37 +178,82 @@
     hits_ref[0] = nn_dot(chosen, scaled_ref[...]).astype(jnp.bfloat16)
 
 
-def totals_kernel(stats_ref, sel_ref, gain_ref, back_ref, loss_ref):
-    total = stats_ref.shape[0]
-    stats = stats_ref[...]
-    gain = gain_ref[...].astype(jnp.float32)
-    sels = [sel_ref[r].astype(jnp.float32) for r in range(MOST)]
-    denom = 0.0
-    target = 0.0
-    for r in range(MOST):
-        denom = denom + jnp.sum(sels[r] * stats[:, r : r + 1], axis=0, keepdims=True)
-        target = target + jnp.sum(
-            sels[r] * stats[:, MOST + r : MOST + r + 1], axis=0, keepdims=True
-        )
-    loss_ref[...] = jnp.log(denom) - target
-    factor = gain / denom
-    lane = lax.broadcasted_iota(jnp.int32, (total, LANES), 1)
-    back = jnp.zeros((total, LANES), jnp.float32)
-    for r in range(MOST):
-        back = jnp.where(lane == r, jnp.sum(sels[r] * factor, axis=1, keepdims=True), back)
-        back = jnp.where(lane == MOST + r, jnp.sum(sels[r] * gain, axis=1, keepdims=True), back)
+def gather_kernel(brief_ref, out_ref):
+    peers = brief_ref.shape[0]
+    copies = out_ref.shape[0]
+    groups = out_ref.shape[1] // 2
+    span = LANES // groups
+    brief = brief_ref[...]
+    lane = lax.broadcasted_iota(jnp.int32, (peers, LANES), 1).astype(jnp.float32)
+    totals, targets = [], []
+    for j in range(groups):
+        total = jnp.zeros((peers, LANES), jnp.float32)
+        target = jnp.zeros((peers, LANES), jnp.float32)
+        for r in range(MOST):
+            at = span * j + r
+            hit = lane == brief[:, at + 2 * MOST : at + 2 * MOST + 1]
+            total = total + jnp.where(hit, brief[:, at : at + 1], 0.0)
+            target = target + jnp.where(hit, brief[:, at + MOST : at + MOST + 1], 0.0)
+        totals.append(jnp.sum(total, axis=0, keepdims=True))
+        targets.append(jnp.sum(target, axis=0, keepdims=True))
+    dense = jnp.concatenate(totals + targets, axis=0)
+    for k in range(copies):
+        out_ref[k] = dense
+
+
+def totals_kernel(dense_ref, brief_ref, back_ref, loss_ref):
+    peers = brief_ref.shape[0]
+    copies, pairs = dense_ref.shape[:2]
+    groups = pairs // 2
+    span = LANES // groups
+    dense = dense_ref[0]
+    for k in range(1, copies):
+        dense = dense + dense_ref[k]
+    denom = dense[:groups]
+    loss_ref[...] = jnp.log(denom) - dense[groups:]
+    brief = brief_ref[...]
+    lane_int = lax.broadcasted_iota(jnp.int32, (peers, LANES), 1)
+    lane = lane_int.astype(jnp.float32)
+    back = jnp.zeros((peers, LANES), jnp.float32)
+    for j in range(groups):
+        for r in range(MOST):
+            at = span * j + r
+            hit = lane == brief[:, at + 2 * MOST : at + 2 * MOST + 1]
+            mine = jnp.sum(jnp.where(hit, denom[j : j + 1], 0.0), axis=1, keepdims=True)
+            back = jnp.where(lane_int == at, mine, back)
     back_ref[...] = back
 
 
-def return_kernel(fac_ref, stats_ref, sums_ref, hits_ref, out_ref, stage):
+def spread(back, total):
+    groups = total // back.shape[0]
+    span = LANES // groups
+    parts = [back]
+    for j in range(1, groups):
+        parts.append(pltpu.roll(back, LANES - span * j, 1))
+    return jnp.concatenate(parts, axis=0)
+
+
+def factor_of(denom, gain):
+    held = gain > 0.0
+    return jnp.where(held, gain / jnp.where(held, denom, 1.0), 0.0)
+
+
+def return_kernel(back_ref, tags_ref, stats_ref, sums_ref, hits_ref, out_ref, stage, denoms):
     some, width = sums_ref.shape[1:]
     segs = width // LANES
-    fac = fac_ref[pl.ds(pl.multiple_of(pl.program_id(0) * some, some), some), :]
+    step = pl.program_id(0)
+
+    @pl.when(step == 0)
+    def _():
+        denoms[...] = spread(back_ref[...], denoms.shape[0])
+
+    denom = denoms[pl.ds(pl.multiple_of(step * some, some), some), :]
     stats = stats_ref[...]
+    tags = tags_ref[...]
     for r in range(MOST):
-        factor = fac[:, r : r + 1]
-        at_label = factor * jnp.exp(stats[:, MOST + r : MOST + r + 1])
-        at_label = at_label - fac[:, MOST + r : MOST + r + 1]
+        gain = tags[:, 4 * r + 3 : 4 * r + 4]
+        factor = factor_of(denom[:, r : r + 1], gain)
+        at_label = factor * jnp.exp(stats[:, MOST + r : MOST + r + 1]) - gain
         grads = factor * sums_ref[r] + at_label * hits_ref[r].astype(jnp.float32)
         for s in range(segs):
             stage[pl.ds(segs * r + s, some, stride=MOST * segs), :] = grads[
@@ -197,16 +262,17 @@
     out_ref[...] = stage[...].astype(jnp.bfloat16)
 
 
-def center_grad_kernel(fac_ref, exps_ref, cols_ref, rows_ref, centers_ref, out_ref):
+def center_grad_kernel(back_ref, exps_ref, tags_ref, rows_ref, centers_ref, out_ref):
     total, count = exps_ref.shape[1:]
-    fac = fac_ref[...]
-    cols = cols_ref[...]
+    denom = spread(back_ref[...], total)
+    tags = tags_ref[...]
     unit_grad = jnp.zeros(out_ref.shape, jnp.float32)
     for r in range(MOST):
-        hit = lax.broadcasted_iota(jnp.int32, (total, count), 1) == cols[:, r : r + 1]
-        weights = fac[:, r : r + 1] * exps_ref[r] - jnp.where(
-            hit, fac[:, MOST + r : MOST + r + 1], 0.0
-        )
+        gain = tags[:, 4 * r + 3 : 4 * r + 4]
+        factor = factor_of(denom[:, r : r + 1], gain)
+        col = 32.0 * tags[:, 4 * r : 4 * r + 1] + tags[:, 4 * r + 1 : 4 * r + 2] - 1.0
+        hit = lax.broadcasted_iota(jnp.int32, (total, count), 1) == col.astype(jnp.int32)
+        weights = factor * exps_ref[r] - jnp.where(hit, gain, 0.0)
         unit_grad = unit_grad + tn_dot(weights.astype(jnp.bfloat16), rows_ref[r])
     unit_grad = LOGIT_SCALE * unit_grad
     c = centers_ref[...].astype(jnp.float32)
@@ -235,11 +301,15 @@
     out_ref[...] = (unit_grad - unit * along) / norm
 
 
-def exchange(x):
-    return lax.all_to_all(x, AXES, split_axis=0, concat_axis=0, tiled=True)
-
-
-def on_device(features, loss_scale, blocks, label_col, block_slot, centers):
+def exchange(x, axes=AXES):
+    return lax.all_to_all(x, axes, split_axis=0, concat_axis=0, tiled=True)
+
+
+def place():
+    return lax.axis_index("z")
+
+
+def on_device(groups, features, loss_scale, blocks, label_col, block_slot, centers):
     samples, width = features.shape
     total = block_slot.shape[0]
     count = centers.shape[0]
@@ -259,6 +329,7 @@
                 features,
                 blocks.T,
                 label_col.reshape(1, samples),
+                loss_scale.reshape(1, samples),
                 block_slot.reshape(1, total),
             )
         ),
@@ -272,15 +343,17 @@
         (centers,),
         (far((count, width), bf16), far((width, count), bf16)),
     )
-    rows_x, exps, cols, stats = call(
+    peers = total // groups
+    rows_x, exps, tags, stats, brief = call(
         "scores",
         scores_kernel,
         (near(payload_in), away(across)),
         (
             far((MOST, total, width), bf16),
             far((MOST, total, count), f32),
-            far((total, LANES), jnp.int32),
             far((total, LANES), f32),
+            far((total, LANES), f32),
+            far((peers, LANES), f32),
         ),
         [here((total * rows, LANES), f32)],
         grid=(MOST,),
@@ -289,13 +362,26 @@
             block((1, total, count), lambda r: (r, 0, 0)),
             block((total, LANES), lambda r: (0, 0)),
             block((total, LANES), lambda r: (0, 0)),
+            block((peers, LANES), lambda r: (0, 0)),
         ),
     )
-    stats_in = exchange(stats.reshape(total, 1, LANES)).reshape(total, LANES)
+    brief_in = exchange(brief.reshape(peers, 1, LANES), PLANE).reshape(peers, LANES)
+    (dense,) = call(
+        "gather", gather_kernel, (near(brief_in),), (far((groups, 2 * groups, LANES), f32),)
+    )
+    dense_in = exchange(dense, ("z",))
+    denoms, losses = call(
+        "totals",
+        totals_kernel,
+        (near(dense_in), near(brief_in)),
+        (far((peers, LANES), f32), far((groups, LANES), f32)),
+    )
+    denoms_in = exchange(denoms.reshape(peers, 1, LANES), PLANE).reshape(peers, LANES)
+    loss = lax.dynamic_index_in_dim(losses, place(), 0, keepdims=False)
     sums, hits = call(
         "partial",
         partial_kernel,
-        (away(exps), away(cols), away(scaled)),
+        (away(exps), away(tags), away(scaled)),
         (far((MOST, total, width), f32), far((MOST, total, width), bf16)),
         grid=(MOST,),
         ins=[block((1, total, count), lambda r: (r, 0, 0)), WHOLE, WHOLE],
@@ -304,22 +390,16 @@
             block((1, total, width), lambda r: (r, 0, 0)),
         ),
     )
-    factors, loss = call(
-        "totals",
-        totals_kernel,
-        (near(stats_in), near(sel), loss_scale.reshape(1, samples)),
-        (far((total, LANES), f32), far((1, samples), f32)),
-    )
-    factors_in = exchange(factors.reshape(total, 1, LANES)).reshape(total, LANES)
     (returned,) = call(
         "returned",
         return_kernel,
-        (near(factors_in), away(stats), away(sums), away(hits)),
+        (near(denoms_in), away(tags), away(stats), away(sums), away(hits)),
         (far((total * back_rows, LANES), bf16),),
-        [here((some * back_rows, LANES), f32)],
+        [here((some * back_rows, LANES), f32), here((total, LANES), f32)],
         grid=(chunks,),
         ins=[
             WHOLE,
+            block((some, LANES), lambda d: (d, 0)),
             block((some, LANES), lambda d: (d, 0)),
             block((MOST, some, width), lambda d: (0, d, 0)),
             block((MOST, some, width), lambda d: (0, d, 0)),
@@ -330,7 +410,7 @@
     (center_grad,) = call(
         "center_grad",
         center_grad_kernel,
-        (near(factors_in), away(exps), away(cols), away(rows_x), away(centers)),
+        (near(denoms_in), away(exps), away(tags), away(rows_x), away(centers)),
         (far((count, width), bf16),),
     )
     (feature_grad,) = call(
@@ -340,10 +420,13 @@
         (far((samples, width), f32),),
         [here((total * back_rows, LANES), f32)],
     )
-    return (loss.reshape(samples), feature_grad, center_grad)
+    return (loss, feature_grad, center_grad)
 
 
 def solution(mesh):
+    groups = 8
+    split = (groups, mesh.shape["dp"] // groups // 2, 2, mesh.shape["grp"])
+    mesh = Mesh(mesh.devices.reshape(split), AXES)
     placed = (
         P(AXES, None),
         P(AXES),
@@ -353,7 +436,7 @@
         P(AXES, None),
     )
     return jax.shard_map(
-        on_device,
+        functools.partial(on_device, groups),
         mesh=mesh,
         in_specs=placed,
         out_specs=(P(AXES), P(AXES, None), P(AXES, None)),

time: 197 us -> 190 us (0.964)
  waiting for transfers between devices: 91.3 us -> 82.5 us
  Pallas kernels: 35.8 us -> 40 us
  starting transfers between devices: 42.1 us -> 38.9 us
    all_to_all x3, waiting for transfers between devices: 91.3 us -> 82.5 us  [exchange(): return lax.all_to_all(x, axes, split_axis=0, concat_axis=0, tiled=True)]
    pallas_call x8 -> x9, Pallas kernels: 35.8 us -> 40 us  [call(): pl.pallas_call(kernel, out_shape=tuple(outs), grid=grid, in_specs=ins or...]
    all_to_all x3, starting transfers between devices: 42.1 us -> 38.9 us  [exchange(): return lax.all_to_all(x, axes, split_axis=0, concat_axis=0, tiled=True)]
    all_to_all x1 -> x2, blocking collectives: 26.2 us -> 25.7 us  [exchange(): return lax.all_to_all(x, axes, split_axis=0, concat_axis=0, tiled=True)]
  transfers between devices with their start and end apart: 3 -> 3, of which waited for: 3 -> 3; matrix products, arithmetic and copies ran while one was open for 0% -> 1% of each run, Pallas kernels for 9% -> 9%
where the time goes in v2:
time: 190 us; the launch traced here: 189 us
  waiting for transfers between devices  82.5 us (43%)
  Pallas kernels  40 us (21%)
  starting transfers between devices  38.9 us (20%)
  blocking collectives  25.7 us (14%)
    all_to_all x3, waiting for transfers between devices, exchange(): return lax.all_to_all(x, axes, split_axis=0, concat_axis=0, tiled=True)  82.5 us
    pallas_call x9, Pallas kernels, call(): pl.pallas_call(kernel, out_shape=tuple(outs), grid=grid, in_specs=ins or...  40 us
    all_to_all x3, starting transfers between devices, exchange(): return lax.all_to_all(x, axes, split_axis=0, concat_axis=0, tiled=True)  38.9 us
    all_to_all x2, blocking collectives, exchange(): return lax.all_to_all(x, axes, split_axis=0, concat_axis=0, tiled=True)  25.7 us
  transfers between devices with their start and end apart: 3, of which 3 were waited for; matrix products, arithmetic and copies ran while one was open for 1% of the time, Pallas kernels for 9%

profile of v2, /device:TPU:1, one launch (start us, length us, event | category | flops | bytes accessed | tf_op | source)
XLA Modules:
  0.0 189.0 jit_solution(2257738162232477050)
XLA Ops:
  0.6 3.7 %dispatch.1 = (bf16[7168,128]{1,0:T(8,128)(2,1)}, bf16[3,512,128]{2,1,0:T(8,128)(2,1)}) custom-call(bf16[128,512]{1,0:T(8,128)(2,1)} %feat_ref.3, s32[8,128]{1,0:T(8,128)} %bitcast.28, s32[1,128]{1,0:T(1,128)} %bitcast.30, bf16[1,128]{1,0:T(2,128)(2,1)} %bitcast.31, s32[1,512]{1,0:T(1,128)} %bitcast.29), custom_call_target="tpu_custom_call" | custom-call | tf_op jit(solution)/shard_map/dispatch/pallas_call | solution.py:43
  4.3 0.0 copy-start
  4.3 22.1 %all-to-all-start = ((bf16[512,7,2,128]{3,2,1,0:T(2,128)(2,1)}), bf16[512,7,2,128]{3,2,1,0:T(2,128)(2,1)S(1)}, u32[]{:S(2)}, u32[]{:S(2)}) async-start(bf16[512,7,2,128]{3,2,1,0:T(2,128)(2,1)} %bitcast.25), calls=%async_computation | async-start | bytes 3670016 | tf_op jit(solution)/shard_map/all_to_all | solution.py:305
  26.5 0.0 copy-done
  26.5 2.1 %normalize.1 = (bf16[1024,512]{1,0:T(8,128)(2,1)}, bf16[512,1024]{1,0:T(8,128)(2,1)}) custom-call(bf16[1024,512]{1,0:T(8,128)(2,1)S(1)} %copy-done), custom_call_target="tpu_custom_call" | custom-call | tf_op jit(solution)/shard_map/normalize/pallas_call | solution.py:43
  28.6 46.5 %all-to-all-done = bf16[512,7,2,128]{3,2,1,0:T(2,128)(2,1)S(1)} async-done(((bf16[512,7,2,128]{3,2,1,0:T(2,128)(2,1)}), bf16[512,7,2,128]{3,2,1,0:T(2,128)(2,1)S(1)}, u32[]{:S(2)}, u32[]{:S(2)}) %all-to-all-start) | async-done | bytes 1835040 | tf_op jit(solution)/shard_map/all_to_all | solution.py:305
  75.1 7.5 %scores.1 = (bf16[3,512,512]{2,1,0:T(8,128)(2,1)}, f32[3,512,1024]{2,1,0:T(8,128)}, f32[512,128]{1,0:T(8,128)}, f32[512,128]{1,0:T(8,128)}, f32[64,128]{1,0:T(8,128)}) custom-call(bf16[7168,128]{1,0:T(8,128)(2,1)S(1)} %bitcast.18, bf16[512,1024]{1,0:T(8,128)(2,1)} %get-tuple-element.17.across_ref), custom_call_target="tpu_custom_call" | custom-call | tf_op jit(solution)/shard_map/scores/pallas_call | solution.py:43
  82.6 15.2 %all_to_all.25 = f32[64,1,128]{2,1,0:T(1,128)S(1)} all-to-all(f32[64,1,128]{2,1,0:T(1,128)} %bitcast.27), channel_id=1, replica_groups=mesh['z'=8,'y'=8,'core'=2,'grp'=4] {'y','core','grp'}, dimensions={0} | all-to-all | bytes 65536 | tf_op jit(solution)/shard_map/all_to_all | solution.py:305
  97.8 1.4 gather.1
  99.3 10.5 %all_to_all.26.dense_ref = f32[8,16,128]{2,1,0:T(8,128)S(1)} all-to-all(f32[8,16,128]{2,1,0:T(8,128)} %gather.1), channel_id=1, replica_groups=mesh['z'=8,'y'=8,'core'=2,'grp'=4] {'z'}, dimensions={0} | all-to-all | bytes 131072 | tf_op jit(solution)/shard_map/all_to_all | solution.py:305
  109.8 2.7 %totals.1 = (f32[64,128]{1,0:T(8,128)}, f32[8,128]{1,0:T(8,128)}) custom-call(f32[8,16,128]{2,1,0:T(8,128)S(1)} %all_to_all.26.dense_ref, f32[64,128]{1,0:T(8,128)S(1)} %bitcast.23), custom_call_target="tpu_custom_call" | custom-call | tf_op jit(solution)/shard_map/totals/pallas_call | solution.py:43
  112.4 6.3 %all-to-all-start.3 = ((f32[64,1,128]{2,1,0:T(1,128)}), f32[64,1,128]{2,1,0:T(1,128)S(1)}, u32[]{:S(2)}, u32[]{:S(2)}) async-start(f32[64,1,128]{2,1,0:T(1,128)} %bitcast.26), calls=%async_computation.3 | async-start | bytes 65536 | tf_op jit(solution)/shard_map/all_to_all | solution.py:305
  118.7 7.2 %partial.1 = (f32[3,512,512]{2,1,0:T(8,128)}, bf16[3,512,512]{2,1,0:T(8,128)(2,1)}) custom-call(f32[3,512,1024]{2,1,0:T(8,128)} %get-tuple-element.23.exps_ref, f32[512,128]{1,0:T(8,128)} %get-tuple-element.21.tags_ref, bf16[1024,512]{1,0:T(8,128)(2,1)} %get-tuple-element.24.scaled_ref), custom_call_target="tpu_custom_call" | custom-call | tf_op jit(solution)/shard_map/partial/pallas_call | solution.py:43
  126.0 2.1 %all-to-all-done.3 = f32[64,1,128]{2,1,0:T(1,128)S(1)} async-done(((f32[64,1,128]{2,1,0:T(1,128)}), f32[64,1,128]{2,1,0:T(1,128)S(1)}, u32[]{:S(2)}, u32[]{:S(2)}) %all-to-all-start.3) | async-done | bytes 32800 | tf_op jit(solution)/shard_map/all_to_all | solution.py:305
  128.0 5.2 %returned.1 = bf16[6144,128]{1,0:T(8,128)(2,1)} custom-call(f32[64,128]{1,0:T(8,128)S(1)} %bitcast.20, f32[512,128]{1,0:T(8,128)} %get-tuple-element.21.tags_ref, f32[512,128]{1,0:T(8,128)} %get-tuple-element.22.stats_ref, f32[3,512,512]{2,1,0:T(8,128)} %get-tuple-element.25.sums_ref, bf16[3,512,512]{2,1,0:T(8,128)(2,1)} %get-tuple-element.26.hits_ref), custom_call_target="tpu_custom_call" | custom-call | tf_op jit(solution)/shard_map/returned/pallas_call | solution.py:43
  133.2 10.4 %all-to-all-start.4 = ((bf16[512,3,4,128]{3,2,1,0:T(4,128)(2,1)}), bf16[512,3,4,128]{3,2,1,0:T(4,128)(2,1)S(1)}, u32[]{:S(2)}, u32[]{:S(2)}) async-start(bf16[512,3,4,128]{3,2,1,0:T(4,128)(2,1)} %bitcast.24), calls=%async_computation.4 | async-start | bytes 3145728 | tf_op jit(solution)/shard_map/all_to_all | solution.py:305
  143.6 1.2 dynamic-slice_bitcast_fusion
  144.8 0.0 copy-start.1
  144.8 7.9 %center_grad.1 = bf16[1024,512]{1,0:T(8,128)(2,1)} custom-call(f32[64,128]{1,0:T(8,128)S(1)} %bitcast.21, f32[3,512,1024]{2,1,0:T(8,128)} %get-tuple-element.23.exps_ref, f32[512,128]{1,0:T(8,128)} %get-tuple-element.21.tags_ref, bf16[3,512,512]{2,1,0:T(8,128)(2,1)} %get-tuple-element.28.rows_ref, bf16[1024,512]{1,0:T(8,128)(2,1)} %centers_ref.3), custom_call_target="tpu_custom_call" | custom-call | tf_op jit(solution)/shard_map/center_grad/pallas_call | solution.py:43
  152.8 34.0 %all-to-all-done.4 = bf16[512,3,4,128]{3,2,1,0:T(4,128)(2,1)S(1)} async-done(((bf16[512,3,4,128]{3,2,1,0:T(4,128)(2,1)}), bf16[512,3,4,128]{3,2,1,0:T(4,128)(2,1)S(1)}, u32[]{:S(2)}, u32[]{:S(2)}) %all-to-all-start.4) | async-done | bytes 1572896 | tf_op jit(solution)/shard_map/all_to_all | solution.py:305
  186.7 0.0 copy-done.1
  186.7 2.3 %combine.1 = f32[128,512]{1,0:T(8,128)} custom-call(bf16[6144,128]{1,0:T(8,128)(2,1)S(1)} %bitcast.19, bf16[3,512,128]{2,1,0:T(8,128)(2,1)S(1)} %copy-done.1, bf16[128,512]{1,0:T(8,128)(2,1)} %feat_ref.3), custom_call_target="tpu_custom_call" | custom-call | tf_op jit(solution)/shard_map/combine/pallas_call | solution.py:43
Async XLA Ops:
  4.3 22.2 %copy-start = (bf16[1024,512]{1,0:T(8,128)(2,1)S(1)}, bf16[1024,512]{1,0:T(8,128)(2,1)}, u32[]{:S(2)}) copy-start(bf16[1024,512]{1,0:T(8,128)(2,1)} %centers_ref.3) | copy-start | bytes 3145732
  4.3 70.8 %all-to-all-start = ((bf16[512,7,2,128]{3,2,1,0:T(2,128)(2,1)}), bf16[512,7,2,128]{3,2,1,0:T(2,128)(2,1)S(1)}, u32[]{:S(2)}, u32[]{:S(2)}) async-start(bf16[512,7,2,128]{3,2,1,0:T(2,128)(2,1)} %bitcast.25), calls=%async_computation | async-start | bytes 3670016 | tf_op jit(solution)/shard_map/all_to_all | solution.py:305
  112.4 15.6 %all-to-all-start.3 = ((f32[64,1,128]{2,1,0:T(1,128)}), f32[64,1,128]{2,1,0:T(1,128)S(1)}, u32[]{:S(2)}, u32[]{:S(2)}) async-start(f32[64,1,128]{2,1,0:T(1,128)} %bitcast.26), calls=%async_computation.3 | async-start | bytes 65536 | tf_op jit(solution)/shard_map/all_to_all | solution.py:305
  133.2 53.5 %all-to-all-start.4 = ((bf16[512,3,4,128]{3,2,1,0:T(4,128)(2,1)}), bf16[512,3,4,128]{3,2,1,0:T(4,128)(2,1)S(1)}, u32[]{:S(2)}, u32[]{:S(2)}) async-start(bf16[512,3,4,128]{3,2,1,0:T(4,128)(2,1)} %bitcast.24), calls=%async_computation.4 | async-start | bytes 3145728 | tf_op jit(solution)/shard_map/all_to_all | solution.py:305
  144.8 41.9 %copy-start.1 = (bf16[3,512,128]{2,1,0:T(8,128)(2,1)S(1)}, bf16[3,512,128]{2,1,0:T(8,128)(2,1)}, u32[]{:S(2)}) copy-start(bf16[3,512,128]{2,1,0:T(8,128)(2,1)} %get-tuple-element.27.sel_ref) | copy-start | bytes 1179652

commit v3 on v2

--- a/solution.py
+++ b/solution.py
@@ -33,6 +33,9 @@
 
 
 WHOLE = pl.BlockSpec(memory_space=pltpu.VMEM)
+
+
+AWAY = pl.BlockSpec(memory_space=pl.ANY)
 
 
 def block(shape, place):
@@ -61,7 +64,7 @@
 
 
 def dispatch_kernel(
-    feat_ref, blocks_ref, label_ref, gain_ref, slot_ref, pay_ref, sel_ref, stage
+    feat_ref, blocks_ref, label_ref, gain_ref, slot_ref, pay_ref, sel_ref, stage, packed, sems
 ):
     samples, width = feat_ref.shape
     total = slot_ref.shape[1]
@@ -95,22 +98,34 @@
     field = lax.broadcasted_iota(jnp.int32, (LANES, samples), 0)
     ids = lax.broadcasted_iota(jnp.int32, (LANES, samples), 1).astype(jnp.float32) + 1.0
     tags = jnp.zeros((total, LANES), jnp.float32)
+    sels = []
     for r in range(MOST):
         sel = jnp.where(rank == float(r), named_at, 0.0)
-        sel_bf = sel.astype(jnp.bfloat16)
-        sel_ref[r] = sel_bf
-        picked = nn_dot(sel_bf, normed)
-        for s in range(segs):
-            stage[pl.ds(segs * r + s, total, stride=rows), :] = picked[
-                :, LANES * s : LANES * (s + 1)
-            ]
+        sels.append(sel.astype(jnp.bfloat16))
+        sel_ref[r] = sels[r]
         own_tags = jnp.where(field == 4 * r, high, jnp.where(field == 4 * r + 1, low, 0.0))
         all_tags = jnp.where(field == 4 * r + 2, ids, jnp.where(field == 4 * r + 3, gain, 0.0))
         tags = tags + nt_dot((sel * own_at).astype(jnp.bfloat16), own_tags.astype(jnp.bfloat16))
-        tags = tags + nt_dot(sel_bf, all_tags.astype(jnp.bfloat16))
-    stage[pl.ds(MOST * segs, total, stride=rows), :] = tags
-    stage[pl.ds(MOST * segs + 1, total, stride=rows), :] = jnp.zeros_like(tags)
-    pay_ref[...] = stage[...].astype(jnp.bfloat16)
+        tags = tags + nt_dot(sels[r], all_tags.astype(jnp.bfloat16))
+    chunks = sems.shape[0]
+    some = total // chunks
+    copies = []
+    for d in range(chunks):
+        for r in range(MOST):
+            picked = nn_dot(sels[r][some * d : some * (d + 1)], normed)
+            for s in range(segs):
+                stage[pl.ds(some * rows * d + segs * r + s, some, stride=rows), :] = picked[
+                    :, LANES * s : LANES * (s + 1)
+                ]
+        last = some * rows * d + MOST * segs
+        stage[pl.ds(last, some, stride=rows), :] = tags[some * d : some * (d + 1)]
+        stage[pl.ds(last + 1, some, stride=rows), :] = jnp.zeros((some, LANES), jnp.float32)
+        part = pl.ds(some * rows * d, some * rows)
+        packed[part, :] = stage[part, :].astype(jnp.bfloat16)
+        copies.append(pltpu.make_async_copy(packed.at[part], pay_ref.at[part], sems.at[d]))
+        copies[d].start()
+    for copy in copies:
+        copy.wait()
 
 
 def centers_kernel(centers_ref, scaled_ref, across_ref):
@@ -121,7 +136,9 @@
     across_ref[...] = scaled.T.astype(jnp.bfloat16)
 
 
-def scores_kernel(pay_ref, across_ref, rows_ref, exps_ref, tags_ref, stats_ref, brief_ref, stage):
+def scores_kernel(
+    pay_ref, far_ref, rows_ref, exps_ref, tags_ref, stats_ref, brief_ref, stage, across_ref, sem
+):
     width, count = across_ref.shape
     segs = width // LANES
     rows = MOST * segs + 2
@@ -132,9 +149,12 @@
 
     @pl.when(r == 0)
     def _():
+        copy = pltpu.make_async_copy(far_ref, across_ref, sem)
+        copy.start()
         stage[...] = pay_ref[...].astype(jnp.float32)
         tags_ref[...] = stage[pl.ds(MOST * segs, total, stride=rows), :]
         stats_ref[...] = jnp.zeros_like(stats_ref)
+        copy.wait()
 
     lane = lax.broadcasted_iota(jnp.int32, (total, LANES), 1)
     shares = jnp.where(lane == 4 * r, 32.0, 0.0) + jnp.where(lane == 4 * r + 1, 1.0, 0.0)
@@ -143,13 +163,21 @@
         [stage[pl.ds(segs * r + s, total, stride=rows), :] for s in range(segs)], axis=1
     ).astype(jnp.bfloat16)
     rows_ref[0] = part
-    scores = nn_dot(part, across_ref[...])
-    hit = lax.broadcasted_iota(jnp.int32, (total, count), 1) == col
-    scores = jnp.where(hit, scores - LOGIT_SCALE * MARGIN, scores)
-    exps = jnp.exp(scores)
-    exps_ref[0] = exps
-    sums = jnp.sum(exps, axis=1, keepdims=True)
-    target = jnp.sum(jnp.where(hit, scores, 0.0), axis=1, keepdims=True)
+    sums = jnp.zeros((total, LANES), jnp.float32)
+    target = jnp.zeros((total, LANES), jnp.float32)
+    wide = 2 * LANES
+    for c in range(0, count, wide):
+        scores = nn_dot(part, across_ref[:, c : c + wide])
+        hit = lax.broadcasted_iota(jnp.int32, (total, wide), 1) == col - c
+        scores = jnp.where(hit, scores - LOGIT_SCALE * MARGIN, scores)
+        exps = jnp.exp(scores)
+        exps_ref[0, :, c : c + wide] = exps.astype(jnp.bfloat16)
+        at_hit = jnp.where(hit, scores, 0.0)
+        for h in range(0, wide, LANES):
+            sums = sums + exps[:, h : h + LANES]
+            target = target + at_hit[:, h : h + LANES]
+    sums = jnp.sum(sums, axis=1, keepdims=True)
+    target = jnp.sum(target, axis=1, keepdims=True)
     stats = jnp.where(lane == r, sums, stats_ref[...])
     stats_ref[...] = jnp.where(lane == MOST + r, target, stats)
 
@@ -172,10 +200,10 @@
     shares = jnp.where(lane == 4 * r, 32.0, 0.0) + jnp.where(lane == 4 * r + 1, 1.0, 0.0)
     col = jnp.sum(tags_ref[...] * shares, axis=1, keepdims=True).astype(jnp.int32) - 1
     hit = lax.broadcasted_iota(jnp.int32, (total, count), 1) == col
-    exps = jnp.where(hit, 0.0, exps_ref[0]).astype(jnp.bfloat16)
-    sums_ref[0] = nn_dot(exps, scaled_ref[...])
+    exps = jnp.where(hit, 0.0, exps_ref[0].astype(jnp.float32)).astype(jnp.bfloat16)
+    sums_ref[r] = nn_dot(exps, scaled_ref[...]).astype(jnp.bfloat16)
     chosen = jnp.where(hit, 1.0, 0.0).astype(jnp.bfloat16)
-    hits_ref[0] = nn_dot(chosen, scaled_ref[...]).astype(jnp.bfloat16)
+    hits_ref[r] = nn_dot(chosen, scaled_ref[...]).astype(jnp.bfloat16)
 
 
 def gather_kernel(brief_ref, out_ref):
@@ -183,20 +211,21 @@
     copies = out_ref.shape[0]
     groups = out_ref.shape[1] // 2
     span = LANES // groups
-    brief = brief_ref[...]
-    lane = lax.broadcasted_iota(jnp.int32, (peers, LANES), 1).astype(jnp.float32)
-    totals, targets = [], []
+    fields = brief_ref[...].T
+    ids = lax.broadcasted_iota(jnp.int32, (LANES, peers), 0).astype(jnp.float32)
+    field = lax.broadcasted_iota(jnp.int32, (LANES, LANES), 1)
+    dense = jnp.zeros((LANES, LANES), jnp.float32)
     for j in range(groups):
-        total = jnp.zeros((peers, LANES), jnp.float32)
-        target = jnp.zeros((peers, LANES), jnp.float32)
+        total = jnp.zeros((LANES, peers), jnp.float32)
+        target = jnp.zeros((LANES, peers), jnp.float32)
         for r in range(MOST):
             at = span * j + r
-            hit = lane == brief[:, at + 2 * MOST : at + 2 * MOST + 1]
-            total = total + jnp.where(hit, brief[:, at : at + 1], 0.0)
-            target = target + jnp.where(hit, brief[:, at + MOST : at + MOST + 1], 0.0)
-        totals.append(jnp.sum(total, axis=0, keepdims=True))
-        targets.append(jnp.sum(target, axis=0, keepdims=True))
-    dense = jnp.concatenate(totals + targets, axis=0)
+            hit = ids == fields[at + 2 * MOST : at + 2 * MOST + 1]
+            total = total + jnp.where(hit, fields[at : at + 1], 0.0)
+            target = target + jnp.where(hit, fields[at + MOST : at + MOST + 1], 0.0)
+        dense = jnp.where(field == j, jnp.sum(total, axis=1, keepdims=True), dense)
+        dense = jnp.where(field == groups + j, jnp.sum(target, axis=1, keepdims=True), dense)
+    dense = dense.T[: 2 * groups]
     for k in range(copies):
         out_ref[k] = dense
 
@@ -211,16 +240,14 @@
         dense = dense + dense_ref[k]
     denom = dense[:groups]
     loss_ref[...] = jnp.log(denom) - dense[groups:]
-    brief = brief_ref[...]
-    lane_int = lax.broadcasted_iota(jnp.int32, (peers, LANES), 1)
-    lane = lane_int.astype(jnp.float32)
+    lane = lax.broadcasted_iota(jnp.int32, (peers, LANES), 1)
+    ids = pltpu.roll(brief_ref[...], LANES - 2 * MOST, 1)
+    ids = jnp.clip(ids, 0.0, LANES - 1.0).astype(jnp.int32)
     back = jnp.zeros((peers, LANES), jnp.float32)
     for j in range(groups):
-        for r in range(MOST):
-            at = span * j + r
-            hit = lane == brief[:, at + 2 * MOST : at + 2 * MOST + 1]
-            mine = jnp.sum(jnp.where(hit, denom[j : j + 1], 0.0), axis=1, keepdims=True)
-            back = jnp.where(lane_int == at, mine, back)
+        row = jnp.broadcast_to(denom[j : j + 1], (peers, LANES))
+        found = jnp.take_along_axis(row, ids, axis=1, mode="promise_in_bounds")
+        back = jnp.where(lane // span == j, found, back)
     back_ref[...] = back
 
 
@@ -239,22 +266,25 @@
 
 
 def return_kernel(back_ref, tags_ref, stats_ref, sums_ref, hits_ref, out_ref, stage, denoms):
-    some, width = sums_ref.shape[1:]
+    some = stats_ref.shape[0]
+    width = sums_ref.shape[2]
     segs = width // LANES
     step = pl.program_id(0)
+    mine = pl.ds(pl.multiple_of(step * some, some), some)
 
     @pl.when(step == 0)
     def _():
         denoms[...] = spread(back_ref[...], denoms.shape[0])
 
-    denom = denoms[pl.ds(pl.multiple_of(step * some, some), some), :]
+    denom = denoms[mine, :]
     stats = stats_ref[...]
     tags = tags_ref[...]
     for r in range(MOST):
         gain = tags[:, 4 * r + 3 : 4 * r + 4]
         factor = factor_of(denom[:, r : r + 1], gain)
         at_label = factor * jnp.exp(stats[:, MOST + r : MOST + r + 1]) - gain
-        grads = factor * sums_ref[r] + at_label * hits_ref[r].astype(jnp.float32)
+        grads = factor * sums_ref[r, mine, :].astype(jnp.float32)
+        grads = grads + at_label * hits_ref[r, mine, :].astype(jnp.float32)
         for s in range(segs):
             stage[pl.ds(segs * r + s, some, stride=MOST * segs), :] = grads[
                 :, LANES * s : LANES * (s + 1)
@@ -262,7 +292,7 @@
     out_ref[...] = stage[...].astype(jnp.bfloat16)
 
 
-def center_grad_kernel(back_ref, exps_ref, tags_ref, rows_ref, centers_ref, out_ref):
+def center_grad_kernel(back_ref, exps_ref, tags_ref, stats_ref, rows_ref, centers_ref, out_ref):
     total, count = exps_ref.shape[1:]
     denom = spread(back_ref[...], total)
     tags = tags_ref[...]
@@ -272,7 +302,8 @@
         factor = factor_of(denom[:, r : r + 1], gain)
         col = 32.0 * tags[:, 4 * r : 4 * r + 1] + tags[:, 4 * r + 1 : 4 * r + 2] - 1.0
         hit = lax.broadcasted_iota(jnp.int32, (total, count), 1) == col.astype(jnp.int32)
-        weights = factor * exps_ref[r] - jnp.where(hit, gain, 0.0)
+        at_label = factor * jnp.exp(stats_ref[:, MOST + r : MOST + r + 1]) - gain
+        weights = jnp.where(hit, at_label, factor * exps_ref[r].astype(jnp.float32))
         unit_grad = unit_grad + tn_dot(weights.astype(jnp.bfloat16), rows_ref[r])
     unit_grad = LOGIT_SCALE * unit_grad
     c = centers_ref[...].astype(jnp.float32)
@@ -282,8 +313,10 @@
     out_ref[...] = ((unit_grad - unit * along) / length).astype(jnp.bfloat16)
 
 
-def combine_kernel(back_ref, sel_ref, feat_ref, out_ref, stage):
+def combine_kernel(back_ref, sel_ref, far_ref, out_ref, stage, feat_ref, sem):
     samples, width = feat_ref.shape
+    copy = pltpu.make_async_copy(far_ref, feat_ref, sem)
+    copy.start()
     total = sel_ref.shape[1]
     segs = width // LANES
     stage[...] = back_ref[...].astype(jnp.float32)
@@ -294,6 +327,7 @@
             axis=1,
         ).astype(jnp.bfloat16)
         unit_grad = unit_grad + tn_dot(sel_ref[r], part)
+    copy.wait()
     x = feat_ref[...].astype(jnp.float32)
     norm = jnp.sqrt(jnp.sum(x * x, axis=1, keepdims=True) + EPSILON)
     unit = x / norm
@@ -334,7 +368,12 @@
             )
         ),
         (far((total * rows, LANES), bf16), far((MOST, total, samples), bf16)),
-        [here((total * rows, LANES), f32)],
+        [
+            here((total * rows, LANES), f32),
+            here((total * rows, LANES), bf16),
+            pltpu.SemaphoreType.DMA((chunks,)),
+        ],
+        to=(AWAY, WHOLE),
     )
     payload_in = exchange(payload.reshape(total, rows // 2, 2, LANES)).reshape(total * rows, LANES)
     scaled, across = call(
@@ -350,13 +389,18 @@
         (near(payload_in), away(across)),
         (
             far((MOST, total, width), bf16),
-            far((MOST, total, count), f32),
+            far((MOST, total, count), bf16),
             far((total, LANES), f32),
             far((total, LANES), f32),
             far((peers, LANES), f32),
         ),
-        [here((total * rows, LANES), f32)],
+        [
+            here((total * rows, LANES), f32),
+            here((width, count), bf16),
+            pltpu.SemaphoreType.DMA,
+        ],
         grid=(MOST,),
+        ins=[WHOLE, AWAY],
         to=(
             block((1, total, width), lambda r: (r, 0, 0)),
             block((1, total, count), lambda r: (r, 0, 0)),
@@ -382,18 +426,14 @@
         "partial",
         partial_kernel,
         (away(exps), away(tags), away(scaled)),
-        (far((MOST, total, width), f32), far((MOST, total, width), bf16)),
+        (here((MOST, total, width), bf16), here((MOST, total, width), bf16)),
         grid=(MOST,),
         ins=[block((1, total, count), lambda r: (r, 0, 0)), WHOLE, WHOLE],
-        to=(
-            block((1, total, width), lambda r: (r, 0, 0)),
-            block((1, total, width), lambda r: (r, 0, 0)),
-        ),
     )
     (returned,) = call(
         "returned",
         return_kernel,
-        (near(denoms_in), away(tags), away(stats), away(sums), away(hits)),
+        (near(denoms_in), away(tags), away(stats), near(sums), near(hits)),
         (far((total * back_rows, LANES), bf16),),
         [here((some * back_rows, LANES), f32), here((total, LANES), f32)],
         grid=(chunks,),
@@ -401,8 +441,8 @@
             WHOLE,
             block((some, LANES), lambda d: (d, 0)),
             block((some, LANES), lambda d: (d, 0)),
-            block((MOST, some, width), lambda d: (0, d, 0)),
-            block((MOST, some, width), lambda d: (0, d, 0)),
+            WHOLE,
+            WHOLE,
         ],
         to=(block((some * back_rows, LANES), lambda d: (d, 0)),),
     )
@@ -410,7 +450,7 @@
     (center_grad,) = call(
         "center_grad",
         center_grad_kernel,
-        (near(denoms_in), away(exps), away(tags), away(rows_x), away(centers)),
+        (near(denoms_in), away(exps), away(tags), away(stats), away(rows_x), away(centers)),
         (far((count, width), bf16),),
     )
     (feature_grad,) = call(
@@ -418,7 +458,12 @@
         combine_kernel,
         (near(back), near(sel), away(features)),
         (far((samples, width), f32),),
-        [here((total * back_rows, LANES), f32)],
+        [
+            here((total * back_rows, LANES), f32),
+            here((samples, width), bf16),
+            pltpu.SemaphoreType.DMA,
+        ],
+        ins=[WHOLE, WHOLE, AWAY],
     )
     return (loss, feature_grad, center_grad)
 

time: 190 us -> 186 us (0.979)
  Pallas kernels: 40 us -> 34.3 us
  waiting for transfers between devices: 82.5 us -> 85 us
    pallas_call x9, Pallas kernels: 40 us -> 34.3 us  [call(): pl.pallas_call(kernel, out_shape=tuple(outs), grid=grid, in_specs=ins or...]
    all_to_all x3, waiting for transfers between devices: 82.5 us -> 85 us  [exchange(): return lax.all_to_all(x, axes, split_axis=0, concat_axis=0, tiled=True)]
  transfers between devices with their start and end apart: 3 -> 3, of which waited for: 3 -> 3; matrix products, arithmetic and copies ran while one was open for 1% -> 1% of each run, Pallas kernels for 9% -> 8%
where the time goes in v3:
time: 186 us; the launch traced here: 185 us
  waiting for transfers between devices  85 us (46%)
  starting transfers between devices  37.8 us (20%)
  Pallas kernels  34.3 us (18%)
  blocking collectives  25.8 us (14%)
    all_to_all x3, waiting for transfers between devices, exchange(): return lax.all_to_all(x, axes, split_axis=0, concat_axis=0, tiled=True)  85 us
    all_to_all x3, starting transfers between devices, exchange(): return lax.all_to_all(x, axes, split_axis=0, concat_axis=0, tiled=True)  37.8 us
    pallas_call x9, Pallas kernels, call(): pl.pallas_call(kernel, out_shape=tuple(outs), grid=grid, in_specs=ins or...  34.3 us
    all_to_all x2, blocking collectives, exchange(): return lax.all_to_all(x, axes, split_axis=0, concat_axis=0, tiled=True)  25.8 us
  transfers between devices with their start and end apart: 3, of which 3 were waited for; matrix products, arithmetic and copies ran while one was open for 1% of the time, Pallas kernels for 8%

profile of v3, /device:TPU:1, one launch (start us, length us, event | category | flops | bytes accessed | tf_op | source)
XLA Modules:
  0.0 185.0 jit_solution(8927342749263312720)
XLA Ops:
  0.6 4.1 %dispatch.1 = (bf16[7168,128]{1,0:T(8,128)(2,1)}, bf16[3,512,128]{2,1,0:T(8,128)(2,1)}) custom-call(bf16[128,512]{1,0:T(8,128)(2,1)} %far_ref.1, s32[8,128]{1,0:T(8,128)} %bitcast.28, s32[1,128]{1,0:T(1,128)} %bitcast.30, bf16[1,128]{1,0:T(2,128)(2,1)} %bitcast.31, s32[1,512]{1,0:T(1,128)} %bitcast.29), custom_call_target="tpu_custom_call" | custom-call | tf_op jit(solution)/shard_map/dispatch/pallas_call | solution.py:46
  4.8 0.0 copy-start
  4.8 22.2 %all-to-all-start = ((bf16[512,7,2,128]{3,2,1,0:T(2,128)(2,1)}), bf16[512,7,2,128]{3,2,1,0:T(2,128)(2,1)S(1)}, u32[]{:S(2)}, u32[]{:S(2)}) async-start(bf16[512,7,2,128]{3,2,1,0:T(2,128)(2,1)} %bitcast.25), calls=%async_computation | async-start | bytes 3670016 | tf_op jit(solution)/shard_map/all_to_all | solution.py:339
  27.0 0.0 copy-done
  27.0 2.2 %normalize.1 = (bf16[1024,512]{1,0:T(8,128)(2,1)}, bf16[512,1024]{1,0:T(8,128)(2,1)}) custom-call(bf16[1024,512]{1,0:T(8,128)(2,1)S(1)} %copy-done), custom_call_target="tpu_custom_call" | custom-call | tf_op jit(solution)/shard_map/normalize/pallas_call | solution.py:46
  29.1 46.5 %all-to-all-done = bf16[512,7,2,128]{3,2,1,0:T(2,128)(2,1)S(1)} async-done(((bf16[512,7,2,128]{3,2,1,0:T(2,128)(2,1)}), bf16[512,7,2,128]{3,2,1,0:T(2,128)(2,1)S(1)}, u32[]{:S(2)}, u32[]{:S(2)}) %all-to-all-start) | async-done | bytes 1835040 | tf_op jit(solution)/shard_map/all_to_all | solution.py:339
  75.6 6.6 %scores.1 = (bf16[3,512,512]{2,1,0:T(8,128)(2,1)}, bf16[3,512,1024]{2,1,0:T(8,128)(2,1)}, f32[512,128]{1,0:T(8,128)}, f32[512,128]{1,0:T(8,128)}, f32[64,128]{1,0:T(8,128)}) custom-call(bf16[7168,128]{1,0:T(8,128)(2,1)S(1)} %bitcast.18, bf16[512,1024]{1,0:T(8,128)(2,1)} %get-tuple-element.17.far_ref), custom_call_target="tpu_custom_call" | custom-call | tf_op jit(solution)/shard_map/scores/pallas_call | solution.py:46
  82.2 15.3 %all_to_all.25 = f32[64,1,128]{2,1,0:T(1,128)S(1)} all-to-all(f32[64,1,128]{2,1,0:T(1,128)} %bitcast.27), channel_id=1, replica_groups=mesh['z'=8,'y'=8,'core'=2,'grp'=4] {'y','core','grp'}, dimensions={0} | all-to-all | bytes 65536 | tf_op jit(solution)/shard_map/all_to_all | solution.py:339
  97.5 1.2 gather.1
  98.6 10.5 %all_to_all.26.dense_ref = f32[8,16,128]{2,1,0:T(8,128)S(1)} all-to-all(f32[8,16,128]{2,1,0:T(8,128)} %gather.1), channel_id=1, replica_groups=mesh['z'=8,'y'=8,'core'=2,'grp'=4] {'z'}, dimensions={0} | all-to-all | bytes 131072 | tf_op jit(solution)/shard_map/all_to_all | solution.py:339
  109.1 0.9 totals.1
  110.1 6.4 %all-to-all-start.3 = ((f32[64,1,128]{2,1,0:T(1,128)}), f32[64,1,128]{2,1,0:T(1,128)S(1)}, u32[]{:S(2)}, u32[]{:S(2)}) async-start(f32[64,1,128]{2,1,0:T(1,128)} %bitcast.26), calls=%async_computation.3 | async-start | bytes 65536 | tf_op jit(solution)/shard_map/all_to_all | solution.py:339
  116.4 5.7 %partial.1 = (bf16[3,512,512]{2,1,0:T(8,128)(2,1)S(1)}, bf16[3,512,512]{2,1,0:T(8,128)(2,1)S(1)}) custom-call(bf16[3,512,1024]{2,1,0:T(8,128)(2,1)} %get-tuple-element.23.exps_ref, f32[512,128]{1,0:T(8,128)} %get-tuple-element.21.tags_ref, bf16[1024,512]{1,0:T(8,128)(2,1)} %get-tuple-element.24.scaled_ref), custom_call_target="tpu_custom_call" | custom-call | tf_op jit(solution)/shard_map/partial/pallas_call | solution.py:46
  122.1 3.6 %all-to-all-done.3 = f32[64,1,128]{2,1,0:T(1,128)S(1)} async-done(((f32[64,1,128]{2,1,0:T(1,128)}), f32[64,1,128]{2,1,0:T(1,128)S(1)}, u32[]{:S(2)}, u32[]{:S(2)}) %all-to-all-start.3) | async-done | bytes 32800 | tf_op jit(solution)/shard_map/all_to_all | solution.py:339
  125.7 4.2 %returned.1 = bf16[6144,128]{1,0:T(8,128)(2,1)} custom-call(f32[64,128]{1,0:T(8,128)S(1)} %bitcast.20, f32[512,128]{1,0:T(8,128)} %get-tuple-element.21.tags_ref, f32[512,128]{1,0:T(8,128)} %get-tuple-element.22.stats_ref, bf16[3,512,512]{2,1,0:T(8,128)(2,1)S(1)} %get-tuple-element.25.sums_ref, bf16[3,512,512]{2,1,0:T(8,128)(2,1)S(1)} %get-tuple-element.26.hits_ref), custom_call_target="tpu_custom_call" | custom-call | tf_op jit(solution)/shard_map/returned/pallas_call | solution.py:46
  130.0 9.3 %all-to-all-start.4 = ((bf16[512,3,4,128]{3,2,1,0:T(4,128)(2,1)}), bf16[512,3,4,128]{3,2,1,0:T(4,128)(2,1)S(1)}, u32[]{:S(2)}, u32[]{:S(2)}) async-start(bf16[512,3,4,128]{3,2,1,0:T(4,128)(2,1)} %bitcast.24), calls=%async_computation.4 | async-start | bytes 3145728 | tf_op jit(solution)/shard_map/all_to_all | solution.py:339
  139.3 1.2 dynamic-slice_bitcast_fusion
  140.5 0.0 copy-start.1
  140.5 7.2 %center_grad.1 = bf16[1024,512]{1,0:T(8,128)(2,1)} custom-call(f32[64,128]{1,0:T(8,128)S(1)} %bitcast.21, bf16[3,512,1024]{2,1,0:T(8,128)(2,1)} %get-tuple-element.23.exps_ref, f32[512,128]{1,0:T(8,128)} %get-tuple-element.21.tags_ref, f32[512,128]{1,0:T(8,128)} %get-tuple-element.22.stats_ref, bf16[3,512,512]{2,1,0:T(8,128)(2,1)} %get-tuple-element.28.rows_ref, ...), custom_call_target="tpu_custom_call" | custom-call | tf_op jit(solution)/shard_map/center_grad/pallas_call | solution.py:46
  147.7 34.9 %all-to-all-done.4 = bf16[512,3,4,128]{3,2,1,0:T(4,128)(2,1)S(1)} async-done(((bf16[512,3,4,128]{3,2,1,0:T(4,128)(2,1)}), bf16[512,3,4,128]{3,2,1,0:T(4,128)(2,1)S(1)}, u32[]{:S(2)}, u32[]{:S(2)}) %all-to-all-start.4) | async-done | bytes 1572896 | tf_op jit(solution)/shard_map/all_to_all | solution.py:339
  182.5 0.0 copy-done.1
  182.5 2.3 %combine.1 = f32[128,512]{1,0:T(8,128)} custom-call(bf16[6144,128]{1,0:T(8,128)(2,1)S(1)} %bitcast.19, bf16[3,512,128]{2,1,0:T(8,128)(2,1)S(1)} %copy-done.1, bf16[128,512]{1,0:T(8,128)(2,1)} %far_ref.1), custom_call_target="tpu_custom_call" | custom-call | tf_op jit(solution)/shard_map/combine/pallas_call | solution.py:46
Async XLA Ops:
  4.8 22.2 %copy-start = (bf16[1024,512]{1,0:T(8,128)(2,1)S(1)}, bf16[1024,512]{1,0:T(8,128)(2,1)}, u32[]{:S(2)}) copy-start(bf16[1024,512]{1,0:T(8,128)(2,1)} %centers_ref.3) | copy-start | bytes 3145732
  4.8 70.8 %all-to-all-start = ((bf16[512,7,2,128]{3,2,1,0:T(2,128)(2,1)}), bf16[512,7,2,128]{3,2,1,0:T(2,128)(2,1)S(1)}, u32[]{:S(2)}, u32[]{:S(2)}) async-start(bf16[512,7,2,128]{3,2,1,0:T(2,128)(2,1)} %bitcast.25), calls=%async_computation | async-start | bytes 3670016 | tf_op jit(solution)/shard_map/all_to_all | solution.py:339
  110.1 15.7 %all-to-all-start.3 = ((f32[64,1,128]{2,1,0:T(1,128)}), f32[64,1,128]{2,1,0:T(1,128)S(1)}, u32[]{:S(2)}, u32[]{:S(2)}) async-start(f32[64,1,128]{2,1,0:T(1,128)} %bitcast.26), calls=%async_computation.3 | async-start | bytes 65536 | tf_op jit(solution)/shard_map/all_to_all | solution.py:339
  130.0 52.6 %all-to-all-start.4 = ((bf16[512,3,4,128]{3,2,1,0:T(4,128)(2,1)}), bf16[512,3,4,128]{3,2,1,0:T(4,128)(2,1)S(1)}, u32[]{:S(2)}, u32[]{:S(2)}) async-start(bf16[512,3,4,128]{3,2,1,0:T(4,128)(2,1)} %bitcast.24), calls=%async_computation.4 | async-start | bytes 3145728 | tf_op jit(solution)/shard_map/all_to_all | solution.py:339
  140.5 42.1 %copy-start.1 = (bf16[3,512,128]{2,1,0:T(8,128)(2,1)S(1)}, bf16[3,512,128]{2,1,0:T(8,128)(2,1)}, u32[]{:S(2)}) copy-start(bf16[3,512,128]{2,1,0:T(8,128)(2,1)} %get-tuple-element.27.sel_ref) | copy-start | bytes 1179652

commit v4 on v3

--- a/solution.py
+++ b/solution.py
@@ -10,6 +10,7 @@
 
 BLOCK = 1024
 MOST = 3
+GAP = 4
 LANES = 128
 MARGIN = 0.35
 LOGIT_SCALE = 64.0
@@ -64,7 +65,7 @@
 
 
 def dispatch_kernel(
-    feat_ref, blocks_ref, label_ref, gain_ref, slot_ref, pay_ref, sel_ref, stage, packed, sems
+    feat_ref, blocks_ref, label_ref, gain_ref, slot_ref, pay_ref, sel_ref, stage
 ):
     samples, width = feat_ref.shape
     total = slot_ref.shape[1]
@@ -98,34 +99,22 @@
     field = lax.broadcasted_iota(jnp.int32, (LANES, samples), 0)
     ids = lax.broadcasted_iota(jnp.int32, (LANES, samples), 1).astype(jnp.float32) + 1.0
     tags = jnp.zeros((total, LANES), jnp.float32)
-    sels = []
     for r in range(MOST):
         sel = jnp.where(rank == float(r), named_at, 0.0)
-        sels.append(sel.astype(jnp.bfloat16))
-        sel_ref[r] = sels[r]
-        own_tags = jnp.where(field == 4 * r, high, jnp.where(field == 4 * r + 1, low, 0.0))
-        all_tags = jnp.where(field == 4 * r + 2, ids, jnp.where(field == 4 * r + 3, gain, 0.0))
+        sel_bf = sel.astype(jnp.bfloat16)
+        sel_ref[r] = sel_bf
+        picked = nn_dot(sel_bf, normed)
+        for s in range(segs):
+            stage[pl.ds(segs * r + s, total, stride=rows), :] = picked[
+                :, LANES * s : LANES * (s + 1)
+            ]
+        own_tags = jnp.where(field == r, high, jnp.where(field == GAP + r, low, 0.0))
+        all_tags = jnp.where(field == 2 * GAP + r, ids, jnp.where(field == 3 * GAP + r, gain, 0.0))
         tags = tags + nt_dot((sel * own_at).astype(jnp.bfloat16), own_tags.astype(jnp.bfloat16))
-        tags = tags + nt_dot(sels[r], all_tags.astype(jnp.bfloat16))
-    chunks = sems.shape[0]
-    some = total // chunks
-    copies = []
-    for d in range(chunks):
-        for r in range(MOST):
-            picked = nn_dot(sels[r][some * d : some * (d + 1)], normed)
-            for s in range(segs):
-                stage[pl.ds(some * rows * d + segs * r + s, some, stride=rows), :] = picked[
-                    :, LANES * s : LANES * (s + 1)
-                ]
-        last = some * rows * d + MOST * segs
-        stage[pl.ds(last, some, stride=rows), :] = tags[some * d : some * (d + 1)]
-        stage[pl.ds(last + 1, some, stride=rows), :] = jnp.zeros((some, LANES), jnp.float32)
-        part = pl.ds(some * rows * d, some * rows)
-        packed[part, :] = stage[part, :].astype(jnp.bfloat16)
-        copies.append(pltpu.make_async_copy(packed.at[part], pay_ref.at[part], sems.at[d]))
-        copies[d].start()
-    for copy in copies:
-        copy.wait()
+        tags = tags + nt_dot(sel_bf, all_tags.astype(jnp.bfloat16))
+    stage[pl.ds(MOST * segs, total, stride=rows), :] = tags
+    stage[pl.ds(MOST * segs + 1, total, stride=rows), :] = jnp.zeros_like(tags)
+    pay_ref[...] = stage[...].astype(jnp.bfloat16)
 
 
 def centers_kernel(centers_ref, scaled_ref, across_ref):
@@ -157,36 +146,37 @@
         copy.wait()
 
     lane = lax.broadcasted_iota(jnp.int32, (total, LANES), 1)
-    shares = jnp.where(lane == 4 * r, 32.0, 0.0) + jnp.where(lane == 4 * r + 1, 1.0, 0.0)
+    shares = jnp.where(lane == r, 32.0, 0.0) + jnp.where(lane == GAP + r, 1.0, 0.0)
     col = jnp.sum(tags_ref[...] * shares, axis=1, keepdims=True).astype(jnp.int32) - 1
     part = jnp.concatenate(
         [stage[pl.ds(segs * r + s, total, stride=rows), :] for s in range(segs)], axis=1
     ).astype(jnp.bfloat16)
     rows_ref[0] = part
+    col_wide = jnp.broadcast_to(col, (total, LANES))
     sums = jnp.zeros((total, LANES), jnp.float32)
-    target = jnp.zeros((total, LANES), jnp.float32)
+    found = jnp.zeros((total, LANES), jnp.float32)
+    first = lax.broadcasted_iota(jnp.int32, (1, LANES), 1)
     wide = 2 * LANES
     for c in range(0, count, wide):
         scores = nn_dot(part, across_ref[:, c : c + wide])
-        hit = lax.broadcasted_iota(jnp.int32, (total, wide), 1) == col - c
-        scores = jnp.where(hit, scores - LOGIT_SCALE * MARGIN, scores)
-        exps = jnp.exp(scores)
-        exps_ref[0, :, c : c + wide] = exps.astype(jnp.bfloat16)
-        at_hit = jnp.where(hit, scores, 0.0)
         for h in range(0, wide, LANES):
-            sums = sums + exps[:, h : h + LANES]
-            target = target + at_hit[:, h : h + LANES]
-    sums = jnp.sum(sums, axis=1, keepdims=True)
-    target = jnp.sum(target, axis=1, keepdims=True)
+            tile = scores[:, h : h + LANES]
+            hit = col_wide == first + (c + h)
+            exps = jnp.where(hit, 0.0, jnp.exp(tile))
+            exps_ref[0, :, c + h : c + h + LANES] = exps.astype(jnp.bfloat16)
+            sums = sums + exps
+            found = jnp.where(hit, tile, found)
+    own = col >= 0
+    target = jnp.sum(found, axis=1, keepdims=True) - LOGIT_SCALE * MARGIN
+    target = jnp.where(own, target, 0.0)
+    sums = jnp.sum(sums, axis=1, keepdims=True) + jnp.where(own, jnp.exp(target), 0.0)
     stats = jnp.where(lane == r, sums, stats_ref[...])
-    stats_ref[...] = jnp.where(lane == MOST + r, target, stats)
+    stats_ref[...] = jnp.where(lane == GAP + r, target, stats)
 
     @pl.when(r == MOST - 1)
     def _():
-        stats = stats_ref[...]
-        for k in range(MOST):
-            ids = tags_ref[:, 4 * k + 2 : 4 * k + 3] - 1.0
-            stats = jnp.where(lane == 2 * MOST + k, ids, stats)
+        is_id = (lane >= 2 * GAP) & (lane < 2 * GAP + MOST)
+        stats = jnp.where(is_id, tags_ref[...] - 1.0, stats_ref[...])
         brief = stats[:peers]
         for j in range(1, total // peers):
             brief = brief + pltpu.roll(stats[peers * j : peers * (j + 1)], span * j, 1)
@@ -197,11 +187,10 @@
     total, count = exps_ref.shape[1:]
     r = pl.program_id(0)
     lane = lax.broadcasted_iota(jnp.int32, (total, LANES), 1)
-    shares = jnp.where(lane == 4 * r, 32.0, 0.0) + jnp.where(lane == 4 * r + 1, 1.0, 0.0)
+    shares = jnp.where(lane == r, 32.0, 0.0) + jnp.where(lane == GAP + r, 1.0, 0.0)
     col = jnp.sum(tags_ref[...] * shares, axis=1, keepdims=True).astype(jnp.int32) - 1
-    hit = lax.broadcasted_iota(jnp.int32, (total, count), 1) == col
-    exps = jnp.where(hit, 0.0, exps_ref[0].astype(jnp.float32)).astype(jnp.bfloat16)
-    sums_ref[r] = nn_dot(exps, scaled_ref[...]).astype(jnp.bfloat16)
+    hit = lax.broadcasted_iota(jnp.int32, (1, count), 1) == col
+    sums_ref[r] = nn_dot(exps_ref[0], scaled_ref[...]).astype(jnp.bfloat16)
     chosen = jnp.where(hit, 1.0, 0.0).astype(jnp.bfloat16)
     hits_ref[r] = nn_dot(chosen, scaled_ref[...]).astype(jnp.bfloat16)
 
@@ -220,9 +209,9 @@
         target = jnp.zeros((LANES, peers), jnp.float32)
         for r in range(MOST):
             at = span * j + r
-            hit = ids == fields[at + 2 * MOST : at + 2 * MOST + 1]
+            hit = ids == fields[at + 2 * GAP : at + 2 * GAP + 1]
             total = total + jnp.where(hit, fields[at : at + 1], 0.0)
-            target = target + jnp.where(hit, fields[at + MOST : at + MOST + 1], 0.0)
+            target = target + jnp.where(hit, fields[at + GAP : at + GAP + 1], 0.0)
         dense = jnp.where(field == j, jnp.sum(total, axis=1, keepdims=True), dense)
         dense = jnp.where(field == groups + j, jnp.sum(target, axis=1, keepdims=True), dense)
     dense = dense.T[: 2 * groups]
@@ -241,7 +230,7 @@
     denom = dense[:groups]
     loss_ref[...] = jnp.log(denom) - dense[groups:]
     lane = lax.broadcasted_iota(jnp.int32, (peers, LANES), 1)
-    ids = pltpu.roll(brief_ref[...], LANES - 2 * MOST, 1)
+    ids = pltpu.roll(brief_ref[...], LANES - 2 * GAP, 1)
     ids = jnp.clip(ids, 0.0, LANES - 1.0).astype(jnp.int32)
     back = jnp.zeros((peers, LANES), jnp.float32)
     for j in range(groups):
@@ -260,9 +249,13 @@
     return jnp.concatenate(parts, axis=0)
 
 
-def factor_of(denom, gain):
+def slot_terms(denom, tags, stats):
+    gain = pltpu.roll(tags, LANES - 3 * GAP, 1)
+    target = pltpu.roll(stats, LANES - GAP, 1)
     held = gain > 0.0
-    return jnp.where(held, gain / jnp.where(held, denom, 1.0), 0.0)
+    factors = jnp.where(held, gain / jnp.where(held, denom, 1.0), 0.0)
+    cols = 32.0 * tags + pltpu.roll(tags, LANES - GAP, 1) - 1.0
+    return factors, factors * jnp.exp(target) - gain, cols
 
 
 def return_kernel(back_ref, tags_ref, stats_ref, sums_ref, hits_ref, out_ref, stage, denoms):
@@ -276,15 +269,10 @@
     def _():
         denoms[...] = spread(back_ref[...], denoms.shape[0])
 
-    denom = denoms[mine, :]
-    stats = stats_ref[...]
-    tags = tags_ref[...]
+    factors, at_labels, _ = slot_terms(denoms[mine, :], tags_ref[...], stats_ref[...])
     for r in range(MOST):
-        gain = tags[:, 4 * r + 3 : 4 * r + 4]
-        factor = factor_of(denom[:, r : r + 1], gain)
-        at_label = factor * jnp.exp(stats[:, MOST + r : MOST + r + 1]) - gain
-        grads = factor * sums_ref[r, mine, :].astype(jnp.float32)
-        grads = grads + at_label * hits_ref[r, mine, :].astype(jnp.float32)
+        grads = factors[:, r : r + 1] * sums_ref[r, mine, :].astype(jnp.float32)
+        grads = grads + at_labels[:, r : r + 1] * hits_ref[r, mine, :].astype(jnp.float32)
         for s in range(segs):
             stage[pl.ds(segs * r + s, some, stride=MOST * segs), :] = grads[
                 :, LANES * s : LANES * (s + 1)
@@ -295,15 +283,13 @@
 def center_grad_kernel(back_ref, exps_ref, tags_ref, stats_ref, rows_ref, centers_ref, out_ref):
     total, count = exps_ref.shape[1:]
     denom = spread(back_ref[...], total)
-    tags = tags_ref[...]
+    factors, at_labels, cols = slot_terms(denom, tags_ref[...], stats_ref[...])
+    cols = cols.astype(jnp.int32)
     unit_grad = jnp.zeros(out_ref.shape, jnp.float32)
     for r in range(MOST):
-        gain = tags[:, 4 * r + 3 : 4 * r + 4]
-        factor = factor_of(denom[:, r : r + 1], gain)
-        col = 32.0 * tags[:, 4 * r : 4 * r + 1] + tags[:, 4 * r + 1 : 4 * r + 2] - 1.0
-        hit = lax.broadcasted_iota(jnp.int32, (total, count), 1) == col.astype(jnp.int32)
-        at_label = factor * jnp.exp(stats_ref[:, MOST + r : MOST + r + 1]) - gain
-        weights = jnp.where(hit, at_label, factor * exps_ref[r].astype(jnp.float32))
+        hit = lax.broadcasted_iota(jnp.int32, (1, count), 1) == cols[:, r : r + 1]
+        weights = factors[:, r : r + 1] * exps_ref[r].astype(jnp.float32)
+        weights = jnp.where(hit, at_labels[:, r : r + 1], weights)
         unit_grad = unit_grad + tn_dot(weights.astype(jnp.bfloat16), rows_ref[r])
     unit_grad = LOGIT_SCALE * unit_grad
     c = centers_ref[...].astype(jnp.float32)
@@ -368,12 +354,7 @@
             )
         ),
         (far((total * rows, LANES), bf16), far((MOST, total, samples), bf16)),
-        [
-            here((total * rows, LANES), f32),
-            here((total * rows, LANES), bf16),
-            pltpu.SemaphoreType.DMA((chunks,)),
-        ],
-        to=(AWAY, WHOLE),
+        [here((total * rows, LANES), f32)],
     )
     payload_in = exchange(payload.reshape(total, rows // 2, 2, LANES)).reshape(total * rows, LANES)
     scaled, across = call(

time: 186 us -> 185 us (level)
  no operation moved by 1% of the time
where the time goes in v4:
time: 185 us; the launch traced here: 184 us
  waiting for transfers between devices  84.8 us (46%)
  starting transfers between devices  37.8 us (20%)
  Pallas kernels  33.6 us (18%)
  blocking collectives  25.7 us (14%)
    all_to_all x3, waiting for transfers between devices, exchange(): return lax.all_to_all(x, axes, split_axis=0, concat_axis=0, tiled=True)  84.8 us
    all_to_all x3, starting transfers between devices, exchange(): return lax.all_to_all(x, axes, split_axis=0, concat_axis=0, tiled=True)  37.8 us
    pallas_call x9, Pallas kernels, call(): pl.pallas_call(kernel, out_shape=tuple(outs), grid=grid, in_specs=ins or...  33.6 us
    all_to_all x2, blocking collectives, exchange(): return lax.all_to_all(x, axes, split_axis=0, concat_axis=0, tiled=True)  25.7 us
  transfers between devices with their start and end apart: 3, of which 3 were waited for; matrix products, arithmetic and copies ran while one was open for 1% of the time, Pallas kernels for 8%

profile of v4, /device:TPU:1, one launch (start us, length us, event | category | flops | bytes accessed | tf_op | source)
XLA Modules:
  0.0 184.0 jit_solution(10034784324664015509)
XLA Ops:
  0.6 3.7 %dispatch.1 = (bf16[7168,128]{1,0:T(8,128)(2,1)}, bf16[3,512,128]{2,1,0:T(8,128)(2,1)}) custom-call(bf16[128,512]{1,0:T(8,128)(2,1)} %far_ref.1, s32[8,128]{1,0:T(8,128)} %bitcast.28, s32[1,128]{1,0:T(1,128)} %bitcast.30, bf16[1,128]{1,0:T(2,128)(2,1)} %bitcast.31, s32[1,512]{1,0:T(1,128)} %bitcast.29), custom_call_target="tpu_custom_call" | custom-call | tf_op jit(solution)/shard_map/dispatch/pallas_call | solution.py:47
  4.3 0.0 copy-start
  4.3 22.1 %all-to-all-start = ((bf16[512,7,2,128]{3,2,1,0:T(2,128)(2,1)}), bf16[512,7,2,128]{3,2,1,0:T(2,128)(2,1)S(1)}, u32[]{:S(2)}, u32[]{:S(2)}) async-start(bf16[512,7,2,128]{3,2,1,0:T(2,128)(2,1)} %bitcast.25), calls=%async_computation | async-start | bytes 3670016 | tf_op jit(solution)/shard_map/all_to_all | solution.py:325
  26.5 0.0 copy-done
  26.5 2.2 %normalize.1 = (bf16[1024,512]{1,0:T(8,128)(2,1)}, bf16[512,1024]{1,0:T(8,128)(2,1)}) custom-call(bf16[1024,512]{1,0:T(8,128)(2,1)S(1)} %copy-done), custom_call_target="tpu_custom_call" | custom-call | tf_op jit(solution)/shard_map/normalize/pallas_call | solution.py:47
  28.6 46.5 %all-to-all-done = bf16[512,7,2,128]{3,2,1,0:T(2,128)(2,1)S(1)} async-done(((bf16[512,7,2,128]{3,2,1,0:T(2,128)(2,1)}), bf16[512,7,2,128]{3,2,1,0:T(2,128)(2,1)S(1)}, u32[]{:S(2)}, u32[]{:S(2)}) %all-to-all-start) | async-done | bytes 1835040 | tf_op jit(solution)/shard_map/all_to_all | solution.py:325
  75.1 6.3 %scores.1 = (bf16[3,512,512]{2,1,0:T(8,128)(2,1)}, bf16[3,512,1024]{2,1,0:T(8,128)(2,1)}, f32[512,128]{1,0:T(8,128)}, f32[512,128]{1,0:T(8,128)}, f32[64,128]{1,0:T(8,128)}) custom-call(bf16[7168,128]{1,0:T(8,128)(2,1)S(1)} %bitcast.18, bf16[512,1024]{1,0:T(8,128)(2,1)} %get-tuple-element.17.far_ref), custom_call_target="tpu_custom_call" | custom-call | tf_op jit(solution)/shard_map/scores/pallas_call | solution.py:47
  81.5 15.3 %all_to_all.25 = f32[64,1,128]{2,1,0:T(1,128)S(1)} all-to-all(f32[64,1,128]{2,1,0:T(1,128)} %bitcast.27), channel_id=1, replica_groups=mesh['z'=8,'y'=8,'core'=2,'grp'=4] {'y','core','grp'}, dimensions={0} | all-to-all | bytes 65536 | tf_op jit(solution)/shard_map/all_to_all | solution.py:325
  96.7 1.2 gather.1
  97.9 10.5 %all_to_all.26.dense_ref = f32[8,16,128]{2,1,0:T(8,128)S(1)} all-to-all(f32[8,16,128]{2,1,0:T(8,128)} %gather.1), channel_id=1, replica_groups=mesh['z'=8,'y'=8,'core'=2,'grp'=4] {'z'}, dimensions={0} | all-to-all | bytes 131072 | tf_op jit(solution)/shard_map/all_to_all | solution.py:325
  108.4 0.9 totals.1
  109.3 6.4 %all-to-all-start.3 = ((f32[64,1,128]{2,1,0:T(1,128)}), f32[64,1,128]{2,1,0:T(1,128)S(1)}, u32[]{:S(2)}, u32[]{:S(2)}) async-start(f32[64,1,128]{2,1,0:T(1,128)} %bitcast.26), calls=%async_computation.3 | async-start | bytes 65536 | tf_op jit(solution)/shard_map/all_to_all | solution.py:325
  115.7 5.9 %partial.1 = (bf16[3,512,512]{2,1,0:T(8,128)(2,1)S(1)}, bf16[3,512,512]{2,1,0:T(8,128)(2,1)S(1)}) custom-call(bf16[3,512,1024]{2,1,0:T(8,128)(2,1)} %get-tuple-element.23.exps_ref, f32[512,128]{1,0:T(8,128)} %get-tuple-element.21.tags_ref, bf16[1024,512]{1,0:T(8,128)(2,1)} %get-tuple-element.24.scaled_ref), custom_call_target="tpu_custom_call" | custom-call | tf_op jit(solution)/shard_map/partial/pallas_call | solution.py:47
  121.6 3.4 %all-to-all-done.3 = f32[64,1,128]{2,1,0:T(1,128)S(1)} async-done(((f32[64,1,128]{2,1,0:T(1,128)}), f32[64,1,128]{2,1,0:T(1,128)S(1)}, u32[]{:S(2)}, u32[]{:S(2)}) %all-to-all-start.3) | async-done | bytes 32800 | tf_op jit(solution)/shard_map/all_to_all | solution.py:325
  125.0 4.0 %returned.1 = bf16[6144,128]{1,0:T(8,128)(2,1)} custom-call(f32[64,128]{1,0:T(8,128)S(1)} %bitcast.20, f32[512,128]{1,0:T(8,128)} %get-tuple-element.21.tags_ref, f32[512,128]{1,0:T(8,128)} %get-tuple-element.22.stats_ref, bf16[3,512,512]{2,1,0:T(8,128)(2,1)S(1)} %get-tuple-element.25.sums_ref, bf16[3,512,512]{2,1,0:T(8,128)(2,1)S(1)} %get-tuple-element.26.hits_ref), custom_call_target="tpu_custom_call" | custom-call | tf_op jit(solution)/shard_map/returned/pallas_call | solution.py:47
  129.0 9.3 %all-to-all-start.4 = ((bf16[512,3,4,128]{3,2,1,0:T(4,128)(2,1)}), bf16[512,3,4,128]{3,2,1,0:T(4,128)(2,1)S(1)}, u32[]{:S(2)}, u32[]{:S(2)}) async-start(bf16[512,3,4,128]{3,2,1,0:T(4,128)(2,1)} %bitcast.24), calls=%async_computation.4 | async-start | bytes 3145728 | tf_op jit(solution)/shard_map/all_to_all | solution.py:325
  138.3 1.2 dynamic-slice_bitcast_fusion
  139.5 0.0 copy-start.1
  139.5 7.1 %center_grad.1 = bf16[1024,512]{1,0:T(8,128)(2,1)} custom-call(f32[64,128]{1,0:T(8,128)S(1)} %bitcast.21, bf16[3,512,1024]{2,1,0:T(8,128)(2,1)} %get-tuple-element.23.exps_ref, f32[512,128]{1,0:T(8,128)} %get-tuple-element.21.tags_ref, f32[512,128]{1,0:T(8,128)} %get-tuple-element.22.stats_ref, bf16[3,512,512]{2,1,0:T(8,128)(2,1)} %get-tuple-element.28.rows_ref, ...), custom_call_target="tpu_custom_call" | custom-call | tf_op jit(solution)/shard_map/center_grad/pallas_call | solution.py:47
  146.7 35.0 %all-to-all-done.4 = bf16[512,3,4,128]{3,2,1,0:T(4,128)(2,1)S(1)} async-done(((bf16[512,3,4,128]{3,2,1,0:T(4,128)(2,1)}), bf16[512,3,4,128]{3,2,1,0:T(4,128)(2,1)S(1)}, u32[]{:S(2)}, u32[]{:S(2)}) %all-to-all-start.4) | async-done | bytes 1572896 | tf_op jit(solution)/shard_map/all_to_all | solution.py:325
  181.6 0.0 copy-done.1
  181.6 2.3 %combine.1 = f32[128,512]{1,0:T(8,128)} custom-call(bf16[6144,128]{1,0:T(8,128)(2,1)S(1)} %bitcast.19, bf16[3,512,128]{2,1,0:T(8,128)(2,1)S(1)} %copy-done.1, bf16[128,512]{1,0:T(8,128)(2,1)} %far_ref.1), custom_call_target="tpu_custom_call" | custom-call | tf_op jit(solution)/shard_map/combine/pallas_call | solution.py:47
Async XLA Ops:
  4.3 22.2 %copy-start = (bf16[1024,512]{1,0:T(8,128)(2,1)S(1)}, bf16[1024,512]{1,0:T(8,128)(2,1)}, u32[]{:S(2)}) copy-start(bf16[1024,512]{1,0:T(8,128)(2,1)} %centers_ref.3) | copy-start | bytes 3145732
  4.3 70.8 %all-to-all-start = ((bf16[512,7,2,128]{3,2,1,0:T(2,128)(2,1)}), bf16[512,7,2,128]{3,2,1,0:T(2,128)(2,1)S(1)}, u32[]{:S(2)}, u32[]{:S(2)}) async-start(bf16[512,7,2,128]{3,2,1,0:T(2,128)(2,1)} %bitcast.25), calls=%async_computation | async-start | bytes 3670016 | tf_op jit(solution)/shard_map/all_to_all | solution.py:325
  109.3 15.7 %all-to-all-start.3 = ((f32[64,1,128]{2,1,0:T(1,128)}), f32[64,1,128]{2,1,0:T(1,128)S(1)}, u32[]{:S(2)}, u32[]{:S(2)}) async-start(f32[64,1,128]{2,1,0:T(1,128)} %bitcast.26), calls=%async_computation.3 | async-start | bytes 65536 | tf_op jit(solution)/shard_map/all_to_all | solution.py:325
  129.0 52.6 %all-to-all-start.4 = ((bf16[512,3,4,128]{3,2,1,0:T(4,128)(2,1)}), bf16[512,3,4,128]{3,2,1,0:T(4,128)(2,1)S(1)}, u32[]{:S(2)}, u32[]{:S(2)}) async-start(bf16[512,3,4,128]{3,2,1,0:T(4,128)(2,1)} %bitcast.24), calls=%async_computation.4 | async-start | bytes 3145728 | tf_op jit(solution)/shard_map/all_to_all | solution.py:325
  139.5 42.1 %copy-start.1 = (bf16[3,512,128]{2,1,0:T(8,128)(2,1)S(1)}, bf16[3,512,128]{2,1,0:T(8,128)(2,1)}, u32[]{:S(2)}) copy-start(bf16[3,512,128]{2,1,0:T(8,128)(2,1)} %get-tuple-element.27.sel_ref) | copy-start | bytes 1179652

commit v5 on v4

--- a/solution.py
+++ b/solution.py
@@ -153,15 +153,15 @@
     ).astype(jnp.bfloat16)
     rows_ref[0] = part
     col_wide = jnp.broadcast_to(col, (total, LANES))
+    tile_of = jnp.where(lane == (col_wide & (LANES - 1)), col_wide >> 7, -1)
     sums = jnp.zeros((total, LANES), jnp.float32)
     found = jnp.zeros((total, LANES), jnp.float32)
-    first = lax.broadcasted_iota(jnp.int32, (1, LANES), 1)
     wide = 2 * LANES
     for c in range(0, count, wide):
         scores = nn_dot(part, across_ref[:, c : c + wide])
         for h in range(0, wide, LANES):
             tile = scores[:, h : h + LANES]
-            hit = col_wide == first + (c + h)
+            hit = tile_of == (c + h) // LANES
             exps = jnp.where(hit, 0.0, jnp.exp(tile))
             exps_ref[0, :, c + h : c + h + LANES] = exps.astype(jnp.bfloat16)
             sums = sums + exps
@@ -338,7 +338,7 @@
     back_rows = MOST * segs
     bf16, f32 = jnp.bfloat16, jnp.float32
     far, here = pltpu.HBM, pltpu.VMEM
-    chunks = 4
+    chunks = 2
     some = total // chunks
     payload, sel = call(
         "dispatch",

time: 185 us -> 183 us (0.989)
  no operation moved by 1% of the time
where the time goes in v5:
time: 183 us
  waiting for transfers between devices  84.8 us (46%)
  starting transfers between devices  37.8 us (21%)
  Pallas kernels  32.3 us (18%)
  blocking collectives  25.7 us (14%)
    all_to_all x3, waiting for transfers between devices, exchange(): return lax.all_to_all(x, axes, split_axis=0, concat_axis=0, tiled=True)  84.8 us
    all_to_all x3, starting transfers between devices, exchange(): return lax.all_to_all(x, axes, split_axis=0, concat_axis=0, tiled=True)  37.8 us
    pallas_call x9, Pallas kernels, call(): pl.pallas_call(kernel, out_shape=tuple(outs), grid=grid, in_specs=ins or...  32.3 us
    all_to_all x2, blocking collectives, exchange(): return lax.all_to_all(x, axes, split_axis=0, concat_axis=0, tiled=True)  25.7 us
  transfers between devices with their start and end apart: 3, of which 3 were waited for; matrix products, arithmetic and copies ran while one was open for 1% of the time, Pallas kernels for 8%

profile of v5, /device:TPU:1, one launch (start us, length us, event | category | flops | bytes accessed | tf_op | source)
XLA Modules:
  0.0 182.7 jit_solution(8367613803807196652)
XLA Ops:
  0.6 3.7 %dispatch.1 = (bf16[7168,128]{1,0:T(8,128)(2,1)}, bf16[3,512,128]{2,1,0:T(8,128)(2,1)}) custom-call(bf16[128,512]{1,0:T(8,128)(2,1)} %far_ref.1, s32[8,128]{1,0:T(8,128)} %bitcast.28, s32[1,128]{1,0:T(1,128)} %bitcast.30, bf16[1,128]{1,0:T(2,128)(2,1)} %bitcast.31, s32[1,512]{1,0:T(1,128)} %bitcast.29), custom_call_target="tpu_custom_call" | custom-call | tf_op jit(solution)/shard_map/dispatch/pallas_call | solution.py:47
  4.3 0.0 copy-start
  4.3 22.1 %all-to-all-start = ((bf16[512,7,2,128]{3,2,1,0:T(2,128)(2,1)}), bf16[512,7,2,128]{3,2,1,0:T(2,128)(2,1)S(1)}, u32[]{:S(2)}, u32[]{:S(2)}) async-start(bf16[512,7,2,128]{3,2,1,0:T(2,128)(2,1)} %bitcast.25), calls=%async_computation | async-start | bytes 3670016 | tf_op jit(solution)/shard_map/all_to_all | solution.py:325
  26.5 0.0 copy-done
  26.5 2.2 %normalize.1 = (bf16[1024,512]{1,0:T(8,128)(2,1)}, bf16[512,1024]{1,0:T(8,128)(2,1)}) custom-call(bf16[1024,512]{1,0:T(8,128)(2,1)S(1)} %copy-done), custom_call_target="tpu_custom_call" | custom-call | tf_op jit(solution)/shard_map/normalize/pallas_call | solution.py:47
  28.6 46.5 %all-to-all-done = bf16[512,7,2,128]{3,2,1,0:T(2,128)(2,1)S(1)} async-done(((bf16[512,7,2,128]{3,2,1,0:T(2,128)(2,1)}), bf16[512,7,2,128]{3,2,1,0:T(2,128)(2,1)S(1)}, u32[]{:S(2)}, u32[]{:S(2)}) %all-to-all-start) | async-done | bytes 1835040 | tf_op jit(solution)/shard_map/all_to_all | solution.py:325
  75.1 6.0 %scores.1 = (bf16[3,512,512]{2,1,0:T(8,128)(2,1)}, bf16[3,512,1024]{2,1,0:T(8,128)(2,1)}, f32[512,128]{1,0:T(8,128)}, f32[512,128]{1,0:T(8,128)}, f32[64,128]{1,0:T(8,128)}) custom-call(bf16[7168,128]{1,0:T(8,128)(2,1)S(1)} %bitcast.18, bf16[512,1024]{1,0:T(8,128)(2,1)} %get-tuple-element.17.far_ref), custom_call_target="tpu_custom_call" | custom-call | tf_op jit(solution)/shard_map/scores/pallas_call | solution.py:47
  81.2 15.3 %all_to_all.25 = f32[64,1,128]{2,1,0:T(1,128)S(1)} all-to-all(f32[64,1,128]{2,1,0:T(1,128)} %bitcast.27), channel_id=1, replica_groups=mesh['z'=8,'y'=8,'core'=2,'grp'=4] {'y','core','grp'}, dimensions={0} | all-to-all | bytes 65536 | tf_op jit(solution)/shard_map/all_to_all | solution.py:325
  96.4 1.2 gather.1
  97.6 10.5 %all_to_all.26.dense_ref = f32[8,16,128]{2,1,0:T(8,128)S(1)} all-to-all(f32[8,16,128]{2,1,0:T(8,128)} %gather.1), channel_id=1, replica_groups=mesh['z'=8,'y'=8,'core'=2,'grp'=4] {'z'}, dimensions={0} | all-to-all | bytes 131072 | tf_op jit(solution)/shard_map/all_to_all | solution.py:325
  108.1 0.9 totals.1
  109.0 6.4 %all-to-all-start.3 = ((f32[64,1,128]{2,1,0:T(1,128)}), f32[64,1,128]{2,1,0:T(1,128)S(1)}, u32[]{:S(2)}, u32[]{:S(2)}) async-start(f32[64,1,128]{2,1,0:T(1,128)} %bitcast.26), calls=%async_computation.3 | async-start | bytes 65536 | tf_op jit(solution)/shard_map/all_to_all | solution.py:325
  115.4 5.9 %partial.1 = (bf16[3,512,512]{2,1,0:T(8,128)(2,1)S(1)}, bf16[3,512,512]{2,1,0:T(8,128)(2,1)S(1)}) custom-call(bf16[3,512,1024]{2,1,0:T(8,128)(2,1)} %get-tuple-element.23.exps_ref, f32[512,128]{1,0:T(8,128)} %get-tuple-element.21.tags_ref, bf16[1024,512]{1,0:T(8,128)(2,1)} %get-tuple-element.24.scaled_ref), custom_call_target="tpu_custom_call" | custom-call | tf_op jit(solution)/shard_map/partial/pallas_call | solution.py:47
  121.3 3.4 %all-to-all-done.3 = f32[64,1,128]{2,1,0:T(1,128)S(1)} async-done(((f32[64,1,128]{2,1,0:T(1,128)}), f32[64,1,128]{2,1,0:T(1,128)S(1)}, u32[]{:S(2)}, u32[]{:S(2)}) %all-to-all-start.3) | async-done | bytes 32800 | tf_op jit(solution)/shard_map/all_to_all | solution.py:325
  124.7 3.0 %returned.1 = bf16[6144,128]{1,0:T(8,128)(2,1)} custom-call(f32[64,128]{1,0:T(8,128)S(1)} %bitcast.20, f32[512,128]{1,0:T(8,128)} %get-tuple-element.21.tags_ref, f32[512,128]{1,0:T(8,128)} %get-tuple-element.22.stats_ref, bf16[3,512,512]{2,1,0:T(8,128)(2,1)S(1)} %get-tuple-element.25.sums_ref, bf16[3,512,512]{2,1,0:T(8,128)(2,1)S(1)} %get-tuple-element.26.hits_ref), custom_call_target="tpu_custom_call" | custom-call | tf_op jit(solution)/shard_map/returned/pallas_call | solution.py:47
  127.7 9.3 %all-to-all-start.4 = ((bf16[512,3,4,128]{3,2,1,0:T(4,128)(2,1)}), bf16[512,3,4,128]{3,2,1,0:T(4,128)(2,1)S(1)}, u32[]{:S(2)}, u32[]{:S(2)}) async-start(bf16[512,3,4,128]{3,2,1,0:T(4,128)(2,1)} %bitcast.24), calls=%async_computation.4 | async-start | bytes 3145728 | tf_op jit(solution)/shard_map/all_to_all | solution.py:325
  137.0 1.2 dynamic-slice_bitcast_fusion
  138.2 0.0 copy-start.1
  138.2 7.1 %center_grad.1 = bf16[1024,512]{1,0:T(8,128)(2,1)} custom-call(f32[64,128]{1,0:T(8,128)S(1)} %bitcast.21, bf16[3,512,1024]{2,1,0:T(8,128)(2,1)} %get-tuple-element.23.exps_ref, f32[512,128]{1,0:T(8,128)} %get-tuple-element.21.tags_ref, f32[512,128]{1,0:T(8,128)} %get-tuple-element.22.stats_ref, bf16[3,512,512]{2,1,0:T(8,128)(2,1)} %get-tuple-element.28.rows_ref, ...), custom_call_target="tpu_custom_call" | custom-call | tf_op jit(solution)/shard_map/center_grad/pallas_call | solution.py:47
  145.3 35.0 %all-to-all-done.4 = bf16[512,3,4,128]{3,2,1,0:T(4,128)(2,1)S(1)} async-done(((bf16[512,3,4,128]{3,2,1,0:T(4,128)(2,1)}), bf16[512,3,4,128]{3,2,1,0:T(4,128)(2,1)S(1)}, u32[]{:S(2)}, u32[]{:S(2)}) %all-to-all-start.4) | async-done | bytes 1572896 | tf_op jit(solution)/shard_map/all_to_all | solution.py:325
  180.3 0.0 copy-done.1
  180.3 2.3 %combine.1 = f32[128,512]{1,0:T(8,128)} custom-call(bf16[6144,128]{1,0:T(8,128)(2,1)S(1)} %bitcast.19, bf16[3,512,128]{2,1,0:T(8,128)(2,1)S(1)} %copy-done.1, bf16[128,512]{1,0:T(8,128)(2,1)} %far_ref.1), custom_call_target="tpu_custom_call" | custom-call | tf_op jit(solution)/shard_map/combine/pallas_call | solution.py:47
Async XLA Ops:
  4.3 22.2 %copy-start = (bf16[1024,512]{1,0:T(8,128)(2,1)S(1)}, bf16[1024,512]{1,0:T(8,128)(2,1)}, u32[]{:S(2)}) copy-start(bf16[1024,512]{1,0:T(8,128)(2,1)} %centers_ref.3) | copy-start | bytes 3145732
  4.3 70.8 %all-to-all-start = ((bf16[512,7,2,128]{3,2,1,0:T(2,128)(2,1)}), bf16[512,7,2,128]{3,2,1,0:T(2,128)(2,1)S(1)}, u32[]{:S(2)}, u32[]{:S(2)}) async-start(bf16[512,7,2,128]{3,2,1,0:T(2,128)(2,1)} %bitcast.25), calls=%async_computation | async-start | bytes 3670016 | tf_op jit(solution)/shard_map/all_to_all | solution.py:325
  109.0 15.7 %all-to-all-start.3 = ((f32[64,1,128]{2,1,0:T(1,128)}), f32[64,1,128]{2,1,0:T(1,128)S(1)}, u32[]{:S(2)}, u32[]{:S(2)}) async-start(f32[64,1,128]{2,1,0:T(1,128)} %bitcast.26), calls=%async_computation.3 | async-start | bytes 65536 | tf_op jit(solution)/shard_map/all_to_all | solution.py:325
  127.7 52.6 %all-to-all-start.4 = ((bf16[512,3,4,128]{3,2,1,0:T(4,128)(2,1)}), bf16[512,3,4,128]{3,2,1,0:T(4,128)(2,1)S(1)}, u32[]{:S(2)}, u32[]{:S(2)}) async-start(bf16[512,3,4,128]{3,2,1,0:T(4,128)(2,1)} %bitcast.24), calls=%async_computation.4 | async-start | bytes 3145728 | tf_op jit(solution)/shard_map/all_to_all | solution.py:325
  138.2 42.1 %copy-start.1 = (bf16[3,512,128]{2,1,0:T(8,128)(2,1)S(1)}, bf16[3,512,128]{2,1,0:T(8,128)(2,1)}, u32[]{:S(2)}) copy-start(bf16[3,512,128]{2,1,0:T(8,128)(2,1)} %get-tuple-element.27.sel_ref) | copy-start | bytes 1179652

commit v6 on v5

--- a/solution.py
+++ b/solution.py
@@ -189,9 +189,11 @@
     lane = lax.broadcasted_iota(jnp.int32, (total, LANES), 1)
     shares = jnp.where(lane == r, 32.0, 0.0) + jnp.where(lane == GAP + r, 1.0, 0.0)
     col = jnp.sum(tags_ref[...] * shares, axis=1, keepdims=True).astype(jnp.int32) - 1
-    hit = lax.broadcasted_iota(jnp.int32, (1, count), 1) == col
     sums_ref[r] = nn_dot(exps_ref[0], scaled_ref[...]).astype(jnp.bfloat16)
-    chosen = jnp.where(hit, 1.0, 0.0).astype(jnp.bfloat16)
+    col_wide = jnp.broadcast_to(col, (total, LANES))
+    tile_of = jnp.where(lane == (col_wide & (LANES - 1)), col_wide >> 7, -1)
+    tiles = [jnp.where(tile_of == t, 1.0, 0.0) for t in range(count // LANES)]
+    chosen = jnp.concatenate(tiles, axis=1).astype(jnp.bfloat16)
     hits_ref[r] = nn_dot(chosen, scaled_ref[...]).astype(jnp.bfloat16)
 
 

time: 183 us -> 183 us (level)
  no operation moved by 1% of the time
where the time goes in v6:
time: 183 us
  waiting for transfers between devices  85.3 us (47%)
  starting transfers between devices  37.8 us (21%)
  Pallas kernels  31.8 us (17%)
  blocking collectives  25.7 us (14%)
    all_to_all x3, waiting for transfers between devices, exchange(): return lax.all_to_all(x, axes, split_axis=0, concat_axis=0, tiled=True)  85.3 us
    all_to_all x3, starting transfers between devices, exchange(): return lax.all_to_all(x, axes, split_axis=0, concat_axis=0, tiled=True)  37.8 us
    pallas_call x9, Pallas kernels, call(): pl.pallas_call(kernel, out_shape=tuple(outs), grid=grid, in_specs=ins or...  31.8 us
    all_to_all x2, blocking collectives, exchange(): return lax.all_to_all(x, axes, split_axis=0, concat_axis=0, tiled=True)  25.7 us
  transfers between devices with their start and end apart: 3, of which 3 were waited for; matrix products, arithmetic and copies ran while one was open for 1% of the time, Pallas kernels for 8%

profile of v6, /device:TPU:1, one launch (start us, length us, event | category | flops | bytes accessed | tf_op | source)
XLA Modules:
  0.0 182.7 jit_solution(7773499721624985627)
XLA Ops:
  0.6 3.7 %dispatch.1 = (bf16[7168,128]{1,0:T(8,128)(2,1)}, bf16[3,512,128]{2,1,0:T(8,128)(2,1)}) custom-call(bf16[128,512]{1,0:T(8,128)(2,1)} %far_ref.1, s32[8,128]{1,0:T(8,128)} %bitcast.28, s32[1,128]{1,0:T(1,128)} %bitcast.30, bf16[1,128]{1,0:T(2,128)(2,1)} %bitcast.31, s32[1,512]{1,0:T(1,128)} %bitcast.29), custom_call_target="tpu_custom_call" | custom-call | tf_op jit(solution)/shard_map/dispatch/pallas_call | solution.py:47
  4.3 0.0 copy-start
  4.3 22.1 %all-to-all-start = ((bf16[512,7,2,128]{3,2,1,0:T(2,128)(2,1)}), bf16[512,7,2,128]{3,2,1,0:T(2,128)(2,1)S(1)}, u32[]{:S(2)}, u32[]{:S(2)}) async-start(bf16[512,7,2,128]{3,2,1,0:T(2,128)(2,1)} %bitcast.25), calls=%async_computation | async-start | bytes 3670016 | tf_op jit(solution)/shard_map/all_to_all | solution.py:327
  26.5 0.0 copy-done
  26.5 2.2 %normalize.1 = (bf16[1024,512]{1,0:T(8,128)(2,1)}, bf16[512,1024]{1,0:T(8,128)(2,1)}) custom-call(bf16[1024,512]{1,0:T(8,128)(2,1)S(1)} %copy-done), custom_call_target="tpu_custom_call" | custom-call | tf_op jit(solution)/shard_map/normalize/pallas_call | solution.py:47
  28.6 46.5 %all-to-all-done = bf16[512,7,2,128]{3,2,1,0:T(2,128)(2,1)S(1)} async-done(((bf16[512,7,2,128]{3,2,1,0:T(2,128)(2,1)}), bf16[512,7,2,128]{3,2,1,0:T(2,128)(2,1)S(1)}, u32[]{:S(2)}, u32[]{:S(2)}) %all-to-all-start) | async-done | bytes 1835040 | tf_op jit(solution)/shard_map/all_to_all | solution.py:327
  75.1 6.0 %scores.1 = (bf16[3,512,512]{2,1,0:T(8,128)(2,1)}, bf16[3,512,1024]{2,1,0:T(8,128)(2,1)}, f32[512,128]{1,0:T(8,128)}, f32[512,128]{1,0:T(8,128)}, f32[64,128]{1,0:T(8,128)}) custom-call(bf16[7168,128]{1,0:T(8,128)(2,1)S(1)} %bitcast.18, bf16[512,1024]{1,0:T(8,128)(2,1)} %get-tuple-element.17.far_ref), custom_call_target="tpu_custom_call" | custom-call | tf_op jit(solution)/shard_map/scores/pallas_call | solution.py:47
  81.2 15.3 %all_to_all.25 = f32[64,1,128]{2,1,0:T(1,128)S(1)} all-to-all(f32[64,1,128]{2,1,0:T(1,128)} %bitcast.27), channel_id=1, replica_groups=mesh['z'=8,'y'=8,'core'=2,'grp'=4] {'y','core','grp'}, dimensions={0} | all-to-all | bytes 65536 | tf_op jit(solution)/shard_map/all_to_all | solution.py:327
  96.4 1.2 gather.1
  97.6 10.5 %all_to_all.26.dense_ref = f32[8,16,128]{2,1,0:T(8,128)S(1)} all-to-all(f32[8,16,128]{2,1,0:T(8,128)} %gather.1), channel_id=1, replica_groups=mesh['z'=8,'y'=8,'core'=2,'grp'=4] {'z'}, dimensions={0} | all-to-all | bytes 131072 | tf_op jit(solution)/shard_map/all_to_all | solution.py:327
  108.1 0.9 totals.1
  109.0 6.4 %all-to-all-start.3 = ((f32[64,1,128]{2,1,0:T(1,128)}), f32[64,1,128]{2,1,0:T(1,128)S(1)}, u32[]{:S(2)}, u32[]{:S(2)}) async-start(f32[64,1,128]{2,1,0:T(1,128)} %bitcast.26), calls=%async_computation.3 | async-start | bytes 65536 | tf_op jit(solution)/shard_map/all_to_all | solution.py:327
  115.4 5.5 %partial.1 = (bf16[3,512,512]{2,1,0:T(8,128)(2,1)S(1)}, bf16[3,512,512]{2,1,0:T(8,128)(2,1)S(1)}) custom-call(bf16[3,512,1024]{2,1,0:T(8,128)(2,1)} %get-tuple-element.23.exps_ref, f32[512,128]{1,0:T(8,128)} %get-tuple-element.21.tags_ref, bf16[1024,512]{1,0:T(8,128)(2,1)} %get-tuple-element.24.scaled_ref), custom_call_target="tpu_custom_call" | custom-call | tf_op jit(solution)/shard_map/partial/pallas_call | solution.py:47
  120.8 3.8 %all-to-all-done.3 = f32[64,1,128]{2,1,0:T(1,128)S(1)} async-done(((f32[64,1,128]{2,1,0:T(1,128)}), f32[64,1,128]{2,1,0:T(1,128)S(1)}, u32[]{:S(2)}, u32[]{:S(2)}) %all-to-all-start.3) | async-done | bytes 32800 | tf_op jit(solution)/shard_map/all_to_all | solution.py:327
  124.7 3.0 %returned.1 = bf16[6144,128]{1,0:T(8,128)(2,1)} custom-call(f32[64,128]{1,0:T(8,128)S(1)} %bitcast.20, f32[512,128]{1,0:T(8,128)} %get-tuple-element.21.tags_ref, f32[512,128]{1,0:T(8,128)} %get-tuple-element.22.stats_ref, bf16[3,512,512]{2,1,0:T(8,128)(2,1)S(1)} %get-tuple-element.25.sums_ref, bf16[3,512,512]{2,1,0:T(8,128)(2,1)S(1)} %get-tuple-element.26.hits_ref), custom_call_target="tpu_custom_call" | custom-call | tf_op jit(solution)/shard_map/returned/pallas_call | solution.py:47
  127.7 9.3 %all-to-all-start.4 = ((bf16[512,3,4,128]{3,2,1,0:T(4,128)(2,1)}), bf16[512,3,4,128]{3,2,1,0:T(4,128)(2,1)S(1)}, u32[]{:S(2)}, u32[]{:S(2)}) async-start(bf16[512,3,4,128]{3,2,1,0:T(4,128)(2,1)} %bitcast.24), calls=%async_computation.4 | async-start | bytes 3145728 | tf_op jit(solution)/shard_map/all_to_all | solution.py:327
  137.0 1.2 dynamic-slice_bitcast_fusion
  138.2 0.0 copy-start.1
  138.2 7.1 %center_grad.1 = bf16[1024,512]{1,0:T(8,128)(2,1)} custom-call(f32[64,128]{1,0:T(8,128)S(1)} %bitcast.21, bf16[3,512,1024]{2,1,0:T(8,128)(2,1)} %get-tuple-element.23.exps_ref, f32[512,128]{1,0:T(8,128)} %get-tuple-element.21.tags_ref, f32[512,128]{1,0:T(8,128)} %get-tuple-element.22.stats_ref, bf16[3,512,512]{2,1,0:T(8,128)(2,1)} %get-tuple-element.28.rows_ref, ...), custom_call_target="tpu_custom_call" | custom-call | tf_op jit(solution)/shard_map/center_grad/pallas_call | solution.py:47
  145.3 35.0 %all-to-all-done.4 = bf16[512,3,4,128]{3,2,1,0:T(4,128)(2,1)S(1)} async-done(((bf16[512,3,4,128]{3,2,1,0:T(4,128)(2,1)}), bf16[512,3,4,128]{3,2,1,0:T(4,128)(2,1)S(1)}, u32[]{:S(2)}, u32[]{:S(2)}) %all-to-all-start.4) | async-done | bytes 1572896 | tf_op jit(solution)/shard_map/all_to_all | solution.py:327
  180.3 0.0 copy-done.1
  180.3 2.3 %combine.1 = f32[128,512]{1,0:T(8,128)} custom-call(bf16[6144,128]{1,0:T(8,128)(2,1)S(1)} %bitcast.19, bf16[3,512,128]{2,1,0:T(8,128)(2,1)S(1)} %copy-done.1, bf16[128,512]{1,0:T(8,128)(2,1)} %far_ref.1), custom_call_target="tpu_custom_call" | custom-call | tf_op jit(solution)/shard_map/combine/pallas_call | solution.py:47
Async XLA Ops:
  4.3 22.2 %copy-start = (bf16[1024,512]{1,0:T(8,128)(2,1)S(1)}, bf16[1024,512]{1,0:T(8,128)(2,1)}, u32[]{:S(2)}) copy-start(bf16[1024,512]{1,0:T(8,128)(2,1)} %centers_ref.3) | copy-start | bytes 3145732
  4.3 70.8 %all-to-all-start = ((bf16[512,7,2,128]{3,2,1,0:T(2,128)(2,1)}), bf16[512,7,2,128]{3,2,1,0:T(2,128)(2,1)S(1)}, u32[]{:S(2)}, u32[]{:S(2)}) async-start(bf16[512,7,2,128]{3,2,1,0:T(2,128)(2,1)} %bitcast.25), calls=%async_computation | async-start | bytes 3670016 | tf_op jit(solution)/shard_map/all_to_all | solution.py:327
  109.0 15.7 %all-to-all-start.3 = ((f32[64,1,128]{2,1,0:T(1,128)}), f32[64,1,128]{2,1,0:T(1,128)S(1)}, u32[]{:S(2)}, u32[]{:S(2)}) async-start(f32[64,1,128]{2,1,0:T(1,128)} %bitcast.26), calls=%async_computation.3 | async-start | bytes 65536 | tf_op jit(solution)/shard_map/all_to_all | solution.py:327
  127.7 52.6 %all-to-all-start.4 = ((bf16[512,3,4,128]{3,2,1,0:T(4,128)(2,1)}), bf16[512,3,4,128]{3,2,1,0:T(4,128)(2,1)S(1)}, u32[]{:S(2)}, u32[]{:S(2)}) async-start(bf16[512,3,4,128]{3,2,1,0:T(4,128)(2,1)} %bitcast.24), calls=%async_computation.4 | async-start | bytes 3145728 | tf_op jit(solution)/shard_map/all_to_all | solution.py:327
  138.2 42.1 %copy-start.1 = (bf16[3,512,128]{2,1,0:T(8,128)(2,1)S(1)}, bf16[3,512,128]{2,1,0:T(8,128)(2,1)}, u32[]{:S(2)}) copy-start(bf16[3,512,128]{2,1,0:T(8,128)(2,1)} %get-tuple-element.27.sel_ref) | copy-start | bytes 1179652
